TPU v7x, 128 devices: a whole 4x4x4 slice. The times are simulated.
128 devices in a mesh: fsdp: 16 (over y, x), sp: 8 (over z, core).
Axes of the slice: x: 4, y: 4, z: 4, core: 2. Of those that a mesh axis runs over, the one named last changes fastest.
Arguments:
- tokens: bfloat16 [16384, 1024], P(('fsdp', 'sp')), may hold values from -6 to 6
- segments: int32 [16, 1024], P('fsdp'), may hold values from 0 to 3, never falling along the last dimension, each value on 1 to 512 neighbouring positions
- top_idx: int32 [16384, 8], P(('fsdp', 'sp')), may hold values from 0 to 15, all different within a row; in each aligned block of 128 rows (0 to 127, 128 to 255, ...) at most 128 rows name the same one
- cotangent: bfloat16 [16384, 1024], P(('fsdp', 'sp')), may hold values from -6 to 6
- norm1_gain: bfloat16 [1024], P(('fsdp', 'sp')), may hold values from 0.099609375 to 1.8984375
- qkv_weight: bfloat16 [1024, 2048], P(('fsdp', 'sp')), may hold values from -0.1875 to 0.1875
- out_weight: bfloat16 [1024, 1024], P(('fsdp', 'sp')), may hold values from -4 to 4
- norm2_gain: bfloat16 [1024], P(('fsdp', 'sp')), may hold values from 0.099609375 to 1.8984375
- router_weight: bfloat16 [1024, 16], P(('fsdp', 'sp')), may hold values from -0.375 to 0.375
- expert_in: bfloat16 [16, 1024, 1024], P('sp', 'fsdp'), may hold values from -0.1875 to 0.1875
- expert_out: bfloat16 [16, 1024, 512], P('sp', 'fsdp'), may hold values from -2 to 2
Outputs:
- block_out: float32 [16384, 1024], P(('fsdp', 'sp'))
- input_grad: float32 [16384, 1024], P(('fsdp', 'sp'))
- norm1_gain_grad: float32 [1024], P(('fsdp', 'sp'))
- qkv_weight_grad: float32 [1024, 2048], P(('fsdp', 'sp'))
- out_weight_grad: float32 [1024, 1024], P(('fsdp', 'sp'))
- norm2_gain_grad: float32 [1024], P(('fsdp', 'sp'))
- router_weight_grad: float32 [1024, 16], P(('fsdp', 'sp'))
- expert_in_grad: float32 [16, 1024, 1024], P('sp', 'fsdp')
- expert_out_grad: float32 [16, 1024, 512], P('sp', 'fsdp')
Inputs may be any that keep to these rules, and one draw needn't show every extreme that they name: `top_idx`: the rows of one device name each expert at most 128 times; the 8 numbers of a row differ. `segments`: each sequence is cut into 4 documents of consecutive positions numbered upward from 0; the longest has 512 positions.
All inputs are finite; a program needn't handle non-finite values.
Results may differ from a plain program's by a relative error of at most 0.02.
Values may be sent and summed in bfloat16 or wider, within the bound.
A program may use at most 128 MiB of HBM per device.

v0:
```python
import jax
import jax.numpy as jnp
import numpy as np
from jax import lax
from jax.experimental import pallas as pl
from jax.experimental.pallas import tpu as pltpu
from jax.sharding import PartitionSpec as P

HQ = 16
KEY_VALUE_HEADS = 8
HEAD_SIZE = 64
E = 16
EPSILON = 1e-06
RESIDUAL = 0.22
BLOCK = 256
LONGEST = 512
BF16 = jnp.bfloat16
F32 = jnp.float32


def rope_tables(count):
    frequency = np.float32(10000.0) ** (
        np.float32(-2.0) * np.arange(HEAD_SIZE // 2, dtype=np.float32) / np.float32(HEAD_SIZE)
    )
    angles = np.arange(count, dtype=np.float32)[:, None] * frequency.astype(np.float32)[None, :]
    cosine = np.cos(angles).astype(np.float32)
    sine = np.sin(angles).astype(np.float32)
    return np.concatenate([cosine] * 4, 1), np.concatenate([-sine, sine] * 2, 1)


def dot(left, right, contract):
    return lax.dot_general(left, right, (contract, ((), ())), preferred_element_type=F32)


def inverse_rms(value):
    return lax.rsqrt(jnp.mean(value * value, -1, keepdims=True) + EPSILON)


def rms_backward(grad, value, inverse, gain):
    scaled = grad * gain
    return inverse * scaled - value * (inverse**3) * jnp.mean(scaled * value, -1, keepdims=True)


MESH = pl.DeviceIdType.MESH
VMEM = pl.BlockSpec(memory_space=pltpu.VMEM)
HBM = pl.BlockSpec(memory_space=pl.ANY)
DMA = pltpu.SemaphoreType.DMA
SP, FSDP = 8, 16


def remote(src, dst, send, recv, **device):
    return pltpu.make_async_remote_copy(
        src_ref=src,
        dst_ref=dst,
        send_sem=send,
        recv_sem=recv,
        device_id=device,
        device_id_type=MESH,
    )


def meet(with_fsdp):
    barrier = pltpu.get_barrier_semaphore()
    me = lax.axis_index("sp")
    for step in range(1, SP):
        pl.semaphore_signal(
            barrier, inc=1, device_id={"sp": lax.rem(me + step, SP)}, device_id_type=MESH
        )
    count = SP - 1
    if with_fsdp:
        size = lax.axis_size("fsdp")
        mine = lax.axis_index("fsdp")
        for step in range(1, size):
            pl.semaphore_signal(
                barrier, inc=1, device_id={"fsdp": lax.rem(mine + step, size)}, device_id_type=MESH
            )
        count += size - 1
    pl.semaphore_wait(barrier, count)


def places():
    me = lax.axis_index("sp")
    level, core = me // 2, lax.rem(me, 2)
    up = lax.rem(level + 1, 4)
    down = lax.rem(level + 3, 4)
    far = lax.rem(level + 2, 4)
    return me, core, level, up, down, far


class Ring:
    def __init__(self, source, slot, part, send, recv, local):
        me, core, level, up, down, far = places()
        self.me = me
        up_id, down_id, far_id = up * 2 + core, down * 2 + core, far * 2 + core
        other = level * 2 + (1 - core)

        def go(src, dst, number, peer):
            return remote(src, dst, send.at[number], recv.at[number], sp=peer)

        self.first = [
            go(source, slot(me), 0, up_id),
            go(source, slot(me), 1, down_id),
            go(source, slot(me), 2, other),
        ]
        self.local = pltpu.make_async_copy(source, slot(me), local)
        self.next_up = [
            go(part(down_id, 0), part(down_id, 0), 3, up_id),
            go(slot(down_id), slot(down_id), 4, other),
        ]
        self.next_down = [
            go(part(up_id, 1), part(up_id, 1), 5, down_id),
            go(slot(up_id), slot(up_id), 6, other),
        ]
        self.last = go(slot(far_id), slot(far_id), 7, other)

    def start(self):
        for copy in self.first:
            copy.start()
        self.local.start()

    def finish(self):
        self.first[0].wait_recv()
        for copy in self.next_up:
            copy.start()
        self.first[1].wait_recv()
        for copy in self.next_down:
            copy.start()
        self.next_up[0].wait_recv()
        self.next_down[0].wait_recv()
        self.last.start()
        self.local.wait()
        for copy in (self.first[0], self.first[1], self.next_up[0], self.next_down[0]):
            copy.wait_send()
        for copy in (self.first[2], self.next_up[1], self.next_down[1], self.last):
            copy.wait()


def ring_rows(source, target, send, recv, local):
    half = source.shape[0] // 2
    return Ring(
        source,
        lambda index: target.at[index],
        lambda index, side: target.at[index, pl.ds(side * half, half)],
        send,
        recv,
        local,
    )


def ring_columns(source, target, send, recv, local):
    rows, wide = source.shape
    half = rows // 2

    def columns(index):
        return pl.ds(pl.multiple_of(index * wide, wide), wide)

    return Ring(
        source,
        lambda index: target.at[:, columns(index)],
        lambda index, side: target.at[pl.ds(side * half, half), columns(index)],
        send,
        recv,
        local,
    )


def spread(axis, size, source, target, send, recv, local, blocks):
    me = lax.axis_index(axis)
    copies = []
    for step in range(1, size):
        peer = lax.rem(me + step, size)
        copies.append(
            remote(
                source.at[peer] if blocks else source,
                target.at[me],
                send.at[step],
                recv.at[step],
                **{axis: peer},
            )
        )
    copies.append(pltpu.make_async_copy(source.at[me] if blocks else source, target.at[me], local))
    return copies


def run(copies):
    for copy in copies:
        copy.start()


def settle(copies):
    for copy in copies:
        copy.wait()


def first_kernel(
    tokens, cotangent, top_idx, qkv, small, outw,
    tokens_all, late_all, mid, packed_all, out_mid,
    packed, late, s0, r0, s1, r1, s2, r2, s3, r3, s4, r4, loc,
):
    group, q_span = 2 * HEAD_SIZE, HQ * HEAD_SIZE
    k_span = KEY_VALUE_HEADS * HEAD_SIZE
    for index in range(SP):
        k_at = q_span + index * HEAD_SIZE
        packed[index, :, :group] = qkv[:, index * group : (index + 1) * group]
        packed[index, :, group : 2 * group] = jnp.concatenate(
            [
                qkv[:, k_at : k_at + HEAD_SIZE],
                qkv[:, k_at + k_span : k_at + k_span + HEAD_SIZE],
            ],
            1,
        )
        packed[index, :, 2 * group :] = small[...]
    meet(True)
    size = lax.axis_size("fsdp")
    small_copies = spread("sp", SP, packed, mid, s1, r1, loc.at[0], True)
    run(small_copies)
    ring = ring_rows(tokens, tokens_all, s0, r0, loc.at[1])
    ring.start()
    width = cotangent.shape[1]
    late[:, :width] = cotangent[...]
    lane = lax.broadcasted_iota(jnp.int32, (cotangent.shape[0], 128), 1)
    chosen = jnp.zeros(lane.shape, F32)
    for choice in range(top_idx.shape[1]):
        chosen = jnp.where(lane == top_idx[:, choice : choice + 1] + 2, 1.0, chosen)
    late[:, width:] = chosen.astype(BF16)
    late_ring = ring_rows(late, late_all, s4, r4, loc.at[4])
    settle(small_copies)
    big = spread("fsdp", size, mid, packed_all, s3, r3, loc.at[3], False)
    run(big)
    out_copies = spread("sp", SP, outw, out_mid, s2, r2, loc.at[2], False)
    run(out_copies)
    late_ring.start()
    ring.finish()
    late_ring.finish()
    settle(out_copies)
    settle(big)


def context_kernel(context, out_mid, context_all, out_all, s0, r0, s1, r1, s2, r2, loc):
    meet(True)
    me, core, level, up, down, far = places()
    size = lax.axis_size("fsdp")
    mine = lax.axis_index("fsdp")
    other = level * 2 + (1 - core)
    keep = pltpu.make_async_copy(out_mid, out_all.at[mine], loc.at[1])
    keep.start()
    sent, passed = [], []
    for step in range(1, size):
        peer = lax.rem(mine + step, size)
        sent.append(
            remote(
                out_mid.at[core], out_all.at[mine, core], s1.at[step], r1.at[step], fsdp=peer
            )
        )
        source = lax.rem(mine + size - step, size)
        passed.append(
            remote(
                out_all.at[source, core],
                out_all.at[source, core],
                s2.at[step],
                r2.at[step],
                sp=other,
            )
        )
    ring = ring_columns(context, context_all, s0, r0, loc.at[0])
    ring.start()
    run(sent)
    ring.finish()
    for copy, onward in zip(sent, passed):
        copy.wait_recv()
        onward.start()
    for copy in sent:
        copy.wait_send()
    settle(passed)
    keep.wait()


def gather_kernel(source, target, send, recv, local):
    meet(False)
    ring = ring_rows(source, target, send, recv, local)
    ring.start()
    ring.finish()


class Scatter:
    def __init__(self, blocks, other_sums, sums, near, far_parts, send, recv):
        me, core, level, up, down, far = places()
        other = level * 2 + (1 - core)
        self.blocks, self.other_sums, self.sums = blocks, other_sums, sums
        self.near, self.far_parts = near, far_parts
        self.core, self.level, self.up, self.down, self.far = core, level, up, down, far
        half = blocks.shape[1] // 2
        self.half = half
        up_id, down_id = up * 2 + core, down * 2 + core

        def go(src, dst, number, peer):
            return remote(src, dst, send.at[number], recv.at[number], sp=peer)

        order = (far, up, down, level)
        self.pair = [
            go(blocks.at[at * 2 + (1 - core)], other_sums.at[number], number, other)
            for number, at in enumerate(order)
        ]
        self.to_up = go(sums.at[0, pl.ds(0, half)], far_parts.at[0], 4, up_id)
        self.to_down = go(sums.at[0, pl.ds(half, half)], far_parts.at[1], 5, down_id)
        self.full_up = go(sums.at[1], near.at[0], 6, up_id)
        self.full_down = go(sums.at[2], near.at[1], 7, down_id)

    def start(self):
        run(self.pair)

    def both(self, number, at):
        mine = self.blocks[at * 2 + self.core].astype(F32)
        return mine + self.other_sums[number].astype(F32)

    def middle(self):
        self.pair[0].wait_recv()
        self.sums[0] = self.both(0, self.far).astype(BF16)
        self.to_up.start()
        self.to_down.start()

    def near_blocks(self):
        half = self.half
        self.pair[1].wait_recv()
        self.to_up.wait_recv()
        total = self.both(1, self.up)
        self.sums[1, :half] = (total[:half] + self.far_parts[0].astype(F32)).astype(BF16)
        self.sums[1, half:] = total[half:].astype(BF16)
        self.full_up.start()
        self.pair[2].wait_recv()
        self.to_down.wait_recv()
        total = self.both(2, self.down)
        self.sums[2, :half] = total[:half].astype(BF16)
        self.sums[2, half:] = (total[half:] + self.far_parts[1].astype(F32)).astype(BF16)
        self.full_down.start()

    def end(self, out):
        self.pair[3].wait_recv()
        total = self.both(3, self.level)
        self.full_up.wait_recv()
        total = total + self.near[0].astype(F32)
        self.full_down.wait_recv()
        out[...] = total + self.near[1].astype(F32)
        for copy in self.pair + [self.to_up, self.to_down, self.full_up, self.full_down]:
            copy.wait_send()

    def finish(self, out):
        self.middle()
        self.near_blocks()
        self.end(out)


def scatter_scratch(rows, width):
    return [
        pltpu.VMEM((4, rows, width), BF16),
        pltpu.VMEM((3, rows, width), BF16),
        pltpu.VMEM((2, rows, width), BF16),
        pltpu.VMEM((2, rows // 2, width), BF16),
        DMA((8,)),
        DMA((8,)),
    ]


def experts_kernel(
    normed, late, small, weights,
    mixed, gates, out, grads,
    w_buf, acts, grad_acts, grad_results, blocks,
    other_sums, sums, near, far_parts, send, recv, loads,
):
    experts, width, both_span = weights.shape
    in_span = 2 * both_span // 3
    hidden = both_span - in_span
    copies = [
        pltpu.make_async_copy(weights.at[local], w_buf.at[local], loads.at[local])
        for local in range(experts)
    ]
    run(copies)
    meet(False)
    sp_index = lax.axis_index("sp")
    settle(copies)
    chunk = 256

    def tokens_block(index, carry):
        at = pl.ds(pl.multiple_of(index * chunk, chunk), chunk)
        rows = normed[at, :]
        logits = dot(rows, small[...], ((1,), (0,)))
        lane = lax.broadcasted_iota(jnp.int32, logits.shape, 1)
        shown = jnp.where(late[at, width:].astype(F32) > 0, logits, -jnp.inf)
        expo = jnp.exp(shown - jnp.max(shown, -1, keepdims=True))
        gate_rows = expo / jnp.sum(expo, -1, keepdims=True)
        gates[at, :] = gate_rows
        grad_mixed = RESIDUAL * late[at, :width].astype(F32)
        mix = jnp.zeros((chunk, width), F32)
        back = jnp.zeros((chunk, width), F32)
        extra = jnp.zeros((chunk, 128), F32)
        for local in range(experts):
            expert = lane == sp_index * experts + local + 2
            gate = jnp.sum(jnp.where(expert, gate_rows, 0.0), -1, keepdims=True)
            pre_act = dot(rows, w_buf[local, :, :in_span], ((1,), (0,)))
            gate_part, up_part = pre_act[:, :hidden], pre_act[:, hidden:]
            sigmoid = 1.0 / (1.0 + jnp.exp(-gate_part))
            silu = gate_part * sigmoid
            act = (silu * up_part).astype(BF16)
            acts[local, at, :] = act
            produced = dot(act, w_buf[local, :, in_span:], ((1,), (1,))).astype(BF16).astype(F32)
            mix = mix + gate * produced
            grad_gate = jnp.sum(grad_mixed * produced, -1, keepdims=True)
            extra = extra + jnp.where(expert, gate * grad_gate, 0.0)
            grad_result = (gate * grad_mixed).astype(BF16)
            grad_results[local, at, :] = grad_result
            grad_act = dot(grad_result, w_buf[local, :, in_span:], ((1,), (0,)))
            grad_gate_part = grad_act * up_part * sigmoid * (1.0 + gate_part * (1.0 - sigmoid))
            grad_pre = jnp.concatenate([grad_gate_part, grad_act * silu], 1).astype(BF16)
            grad_acts[local, at, :] = grad_pre
            back = back + dot(grad_pre, w_buf[local, :, :in_span], ((1,), (1,)))
        mixed[at, :] = mix.astype(BF16)
        per_block = blocks.shape[1]
        count = chunk // per_block
        for piece in range(count):
            place = slice(piece * per_block, (piece + 1) * per_block)
            blocks[index * count + piece, :, :width] = back[place].astype(BF16)
            blocks[index * count + piece, :, width:] = extra[place].astype(BF16)
        return carry

    lax.fori_loop(0, normed.shape[0] // chunk, tokens_block, 0)
    scatter = Scatter(blocks, other_sums, sums, near, far_parts, send, recv)
    scatter.start()
    owners = grads.shape[0]
    share = width // owners
    tile = 256
    count = tile // share

    def weight_tile(index, carry):
        columns = pl.ds(pl.multiple_of(index * tile, tile), tile)
        turned = normed[:, columns]
        for local in range(experts):
            value = dot(turned, grad_acts[local], ((0,), (0,))).astype(BF16)
            grads[pl.ds(index * count, count), local, :, :in_span] = value.reshape(
                count, share, in_span
            )
            value = dot(grad_results[local, :, columns], acts[local], ((0,), (0,))).astype(BF16)
            grads[pl.ds(index * count, count), local, :, in_span:] = value.reshape(
                count, share, hidden
            )
        return carry

    tiles = width // tile
    lax.fori_loop(0, tiles // 4, weight_tile, 0)
    scatter.middle()
    lax.fori_loop(tiles // 4, tiles // 2, weight_tile, 0)
    scatter.near_blocks()
    lax.fori_loop(tiles // 2, tiles, weight_tile, 0)
    scatter.end(out)


class Quad:
    def __init__(self, axis, source, far_parts, near, sums, send, recv):
        mine = lax.axis_index("fsdp")
        y, x = mine // 4, lax.rem(mine, 4)
        here = x if axis == "x" else y
        self.source, self.far_parts, self.near, self.sums = source, far_parts, near, sums
        self.here = here
        self.up, self.down, self.far = (lax.rem(here + step, 4) for step in (1, 3, 2))

        def device(place):
            return y * 4 + place if axis == "x" else place * 4 + x

        def go(src, dst, number, place):
            return remote(src, dst, send.at[number], recv.at[number], fsdp=device(place))

        self.far_up = go(source(self.far, 0), far_parts.at[0], 0, self.up)
        self.far_down = go(source(self.far, 1), far_parts.at[1], 1, self.down)
        self.plain_up = go(source(self.up, 1), near.at[0, 1], 2, self.up)
        self.plain_down = go(source(self.down, 0), near.at[1, 0], 3, self.down)
        self.sum_up = go(sums.at[0], near.at[0, 0], 4, self.up)
        self.sum_down = go(sums.at[1], near.at[1, 1], 5, self.down)

    def start(self):
        run((self.far_up, self.far_down, self.plain_up, self.plain_down))

    def near_blocks(self):
        self.far_up.wait_recv()
        total = self.source(self.up, 0)[...].astype(F32) + self.far_parts[0].astype(F32)
        self.sums[0] = total.astype(BF16)
        self.sum_up.start()
        self.far_down.wait_recv()
        total = self.source(self.down, 1)[...].astype(F32) + self.far_parts[1].astype(F32)
        self.sums[1] = total.astype(BF16)
        self.sum_down.start()

    def end(self, store):
        for copy in (self.plain_up, self.plain_down, self.sum_up, self.sum_down):
            copy.wait_recv()
        for side in range(2):
            total = self.source(self.here, side)[...].astype(F32)
            total = total + self.near[0, side].astype(F32) + self.near[1, side].astype(F32)
            store(side, total)
        for copy in (
            self.far_up, self.far_down, self.plain_up, self.plain_down, self.sum_up, self.sum_down
        ):
            copy.wait_send()


def quad_scratch(shape):
    return [
        pltpu.VMEM((2,) + shape, BF16),
        pltpu.VMEM((2, 2) + shape, BF16),
        pltpu.VMEM((2,) + shape, BF16),
        DMA((6,)),
        DMA((6,)),
    ]


def exact_dot(left, right, contract):
    return lax.dot_general(
        left, right, (contract, ((), ())), precision=lax.Precision.HIGHEST,
        preferred_element_type=F32,
    )


def back_kernel(
    back, gates, normed, middle, cotangent, gain, small, out_own, context,
    query, key2, value2, sums, cosine, sine, seg_column, seg_row, qkv_own, normed_one,
    grads, mixed,
    grad_middle, grad_normed_one, bundle_all, out_sum, expert_grads, mixed_own,
    attended, attended_all, grad_context, grad_proj, grad_key, grad_value, blocks, small_part,
    bundle, outp, bundle_in, out_in, bundle_sum, halves_a, halves_b,
    *scratch,
):
    scratch = list(scratch)

    def take(count):
        taken = scratch[:count]
        del scratch[:count]
        return taken

    mix_scatter = Scatter(mixed, *take(6))
    scatter = Scatter(blocks, *take(6))

    def half_a(index, side):
        return grads.at[:, index, 0, pl.ds(side * half, half)]

    def half_b(index, side):
        return grads.at[index, :, 1, pl.ds(side * half, half)]

    half = grads.shape[3] // 2
    first_a = Quad("x", half_a, *take(5))
    first_b = Quad("y", half_b, *take(5))
    second_a = Quad("y", lambda index, side: halves_a.at[side, index], *take(5))
    second_b = Quad("x", lambda index, side: halves_b.at[side, index], *take(5))
    ring_send, ring_recv, s1, r1, s2, r2, s3, r3, loc = take(9)

    def keep_a(side, total):
        halves_a[side] = total.astype(BF16)

    def keep_b(side, total):
        halves_b[side] = total.astype(BF16)

    meet(True)
    size = lax.axis_size("fsdp")
    first_a.start()
    first_b.start()
    width = cotangent.shape[1]
    value = middle[...]
    inverse = inverse_rms(value)
    weighted = back[:, width:]
    grad_logits = weighted - gates[...] * jnp.sum(weighted, -1, keepdims=True)
    grad_normed = back[:, :width] + exact_dot(grad_logits, small[...].astype(F32), ((1,), (1,)))
    grad_rows = cotangent[...].astype(F32) + rms_backward(grad_normed, value, inverse, gain[...])
    grad_middle[...] = grad_rows
    attended[...] = (RESIDUAL * grad_rows).astype(BF16)
    ring = ring_rows(attended, attended_all, ring_send, ring_recv, loc.at[0])
    ring.start()
    gain_lane = lax.broadcasted_iota(jnp.int32, grad_logits.shape, 1) == 1
    small_part[...] = exact_dot(normed[...].astype(F32), grad_logits, ((0,), (0,))) + exact_dot(
        grad_normed * value * inverse, gain_lane.astype(F32), ((0,), (0,))
    )
    ring.finish()
    mix_scatter.start()
    first_a.near_blocks()
    first_b.near_blocks()
    rows = attended.shape[0]
    for index in range(SP):
        at = slice(index * rows, (index + 1) * rows)
        grad_context[at, :] = dot(attended_all[index], out_own[...], ((1,), (1,))).astype(BF16)
    out_part = jnp.zeros((context.shape[1], width), F32)
    for index in range(SP):
        at = slice(index * rows, (index + 1) * rows)
        out_part = out_part + dot(context[at, :], attended_all[index], ((0,), (0,)))
    outp[...] = out_part.astype(BF16).reshape(outp.shape)
    outs = spread("fsdp", size, outp, out_in, s2, r2, loc.at[1], True)
    run(outs)
    mix_scatter.middle()
    attention_back_kernel(
        query, key2, value2, sums, grad_context, cosine, sine, seg_column, seg_row,
        grad_proj, grad_key, grad_value,
    )
    mix_scatter.near_blocks()
    span = grad_proj.shape[1]
    share = bundle.shape[1]
    tile = 256
    for index in range(width // tile):
        at = slice(index * tile, (index + 1) * tile)
        part = dot(normed_one[:, at], grad_proj[...], ((0,), (0,))).astype(BF16)
        place = slice(index * tile // share, (index + 1) * tile // share)
        bundle[place, :, :span] = part.reshape(tile // share, share, span)
        bundle[place, :, span:] = small_part[at, :].astype(BF16).reshape(tile // share, share, 128)
    bundles = spread("fsdp", size, bundle, bundle_in, s1, r1, loc.at[2], True)
    run(bundles)
    for index in range(SP):
        at = slice(index * rows, (index + 1) * rows)
        blocks[index] = dot(grad_proj[at, :], qkv_own[...], ((1,), (1,))).astype(BF16)
    scatter.start()
    first_a.end(keep_a)
    first_b.end(keep_b)
    second_a.start()
    second_b.start()
    scatter.middle()
    mix_scatter.end(mixed_own)
    scatter.near_blocks()
    settle(bundles)
    total = bundle_in[0].astype(F32)
    for index in range(1, size):
        total = total + bundle_in[index].astype(F32)
    bundle_sum[...] = total.reshape(bundle_sum.shape)
    shares = spread("sp", SP, bundle_sum, bundle_all, s3, r3, loc.at[3], True)
    run(shares)
    second_a.near_blocks()
    second_b.near_blocks()
    settle(outs)
    total = out_in[0].astype(F32)
    for index in range(1, size):
        total = total + out_in[index].astype(F32)
    out_sum[...] = total

    def store_a(side, total):
        expert_grads[0, side * half : (side + 1) * half, :] = total

    def store_b(side, total):
        expert_grads[1, side * half : (side + 1) * half, :] = total

    second_a.end(store_a)
    second_b.end(store_b)
    scatter.end(grad_normed_one)
    settle(shares)


def wide_call(kernel, name, number, inputs, in_specs, outs, out_specs, scratch):
    return pl.pallas_call(
        kernel,
        name=name,
        out_shape=outs,
        in_specs=in_specs,
        out_specs=out_specs,
        scratch_shapes=scratch,
        cost_estimate=pl.CostEstimate(
            flops=2 * 10**10, bytes_accessed=2 * 10**7, transcendentals=0
        ),
        compiler_params=pltpu.CompilerParams(
            collective_id=number, has_side_effects=True, vmem_limit_bytes=56 * 2**20
        ),
    )(*inputs)


def local_call(kernel, name, inputs, outs, scratch=(), flops=0):
    moved = sum(array.size * array.dtype.itemsize for array in inputs)
    return pl.pallas_call(
        kernel,
        name=name,
        out_shape=outs,
        in_specs=[VMEM] * len(inputs),
        out_specs=jax.tree.map(lambda _: VMEM, outs),
        scratch_shapes=scratch,
        cost_estimate=pl.CostEstimate(flops=flops, bytes_accessed=moved, transcendentals=0),
        compiler_params=pltpu.CompilerParams(vmem_limit_bytes=48 * 2**20),
    )(*inputs)


def swap_halves(value):
    wide = value.shape[-1]
    lane = lax.broadcasted_iota(jnp.int32, value.shape, 1)
    return jnp.where(
        lane % HEAD_SIZE < HEAD_SIZE // 2,
        pltpu.roll(value, wide - HEAD_SIZE // 2, 1),
        pltpu.roll(value, HEAD_SIZE // 2, 1),
    )


def first_head(shape):
    return lax.broadcasted_iota(jnp.int32, shape, 1) < HEAD_SIZE


def stack_heads(slab):
    is_first = first_head(slab.shape)
    zero = jnp.zeros_like(slab)
    return jnp.concatenate([jnp.where(is_first, slab, zero), jnp.where(is_first, zero, slab)], 0)


def merge_heads(stacked):
    half = stacked.shape[0] // 2
    return jnp.where(first_head((half, stacked.shape[1])), stacked[:half], stacked[half:])


def block_scores(block, query2, key2, seg_column, seg_row):
    lo, hi = block * BLOCK, (block + 1) * BLOCK
    k_lo = max(0, lo - LONGEST)
    rows = lo + lax.broadcasted_iota(jnp.int32, (BLOCK, hi - k_lo), 0)
    keys = k_lo + lax.broadcasted_iota(jnp.int32, (BLOCK, hi - k_lo), 1)
    allowed = (keys <= rows) & (seg_column[lo:hi, :] == seg_row[:, k_lo:hi])
    scores = dot(query2, key2[k_lo:hi, :], ((1,), (1,))) * HEAD_SIZE**-0.5
    return jnp.where(jnp.concatenate([allowed, allowed], 0), scores, -jnp.inf)


def attention_kernel(
    proj, cosine, sine, seg_column, seg_row, context, query, key2, value2, sums
):
    cos_rows, sin_rows = cosine[...], sine[...]
    slab = proj[:, :128]
    query[...] = (slab * cos_rows + swap_halves(slab) * sin_rows).astype(BF16)
    slab = proj[:, 128:]
    is_first = first_head(slab.shape)
    turned = slab * cos_rows + swap_halves(slab) * sin_rows
    key2[...] = jnp.where(is_first, turned, pltpu.roll(turned, HEAD_SIZE, 1)).astype(BF16)
    value2[...] = jnp.where(is_first, pltpu.roll(slab, HEAD_SIZE, 1), slab).astype(BF16)
    for block in range(proj.shape[0] // BLOCK):
        lo, hi = block * BLOCK, (block + 1) * BLOCK
        k_lo = max(0, lo - LONGEST)
        scores = block_scores(block, stack_heads(query[lo:hi, :]), key2, seg_column, seg_row)
        top = jnp.max(scores, -1, keepdims=True)
        expo = jnp.exp(scores - top)
        total = jnp.sum(expo, -1, keepdims=True)
        probs = (expo / total).astype(BF16)
        context[lo:hi, :] = merge_heads(dot(probs, value2[k_lo:hi, :], ((1,), (0,)))).astype(BF16)
        sums[block] = jnp.broadcast_to(top + jnp.log(total), (2 * BLOCK, 128))


def attention_back_kernel(
    query, key2, value2, sums, grad_context, cosine, sine, seg_column, seg_row,
    grad_proj, grad_key, grad_value,
):
    grad_key[...] = jnp.zeros_like(grad_key)
    grad_value[...] = jnp.zeros_like(grad_value)
    for block in range(query.shape[0] // BLOCK):
        lo, hi = block * BLOCK, (block + 1) * BLOCK
        k_lo = max(0, lo - LONGEST)
        query2 = stack_heads(query[lo:hi, :])
        scores = block_scores(block, query2, key2, seg_column, seg_row)
        probs = jnp.exp(scores - sums[block][:, :1])
        grad_rows = stack_heads(grad_context[lo:hi, :])
        grad_probs = dot(grad_rows, value2[k_lo:hi, :], ((1,), (1,)))
        row_dot = jnp.sum(grad_probs * probs, -1, keepdims=True)
        grad_scores = (probs * (grad_probs - row_dot) * HEAD_SIZE**-0.5).astype(BF16)
        moved = merge_heads(dot(grad_scores, key2[k_lo:hi, :], ((1,), (0,))))
        moved = moved.astype(BF16).astype(F32)
        grad_proj[lo:hi, :128] = (
            moved * cosine[lo:hi, :] - swap_halves(moved) * sine[lo:hi, :]
        ).astype(BF16)
        grad_key[k_lo:hi, :] += dot(grad_scores, query2, ((0,), (0,)))
        grad_value[k_lo:hi, :] += dot(probs.astype(BF16), grad_rows, ((0,), (0,)))
    is_first = first_head(grad_key.shape)
    moved = grad_key[...]
    moved = (moved + pltpu.roll(moved, HEAD_SIZE, 1)).astype(BF16).astype(F32)
    moved = moved * cosine[...] - swap_halves(moved) * sine[...]
    other = grad_value[...]
    other = other + pltpu.roll(other, HEAD_SIZE, 1)
    grad_proj[:, 128:] = jnp.where(is_first, moved, other).astype(BF16)


def shards(
    tokens,
    segments,
    top_idx,
    cotangent,
    norm1_gain,
    qkv_weight,
    out_weight,
    norm2_gain,
    router_weight,
    expert_in,
    expert_out,
):
    n_sp = lax.axis_size("sp")
    n_fsdp = lax.axis_size("fsdp")
    sp_index = lax.axis_index("sp")
    rows, width = tokens.shape
    seq_len = rows * n_sp
    weight_rows = qkv_weight.shape[0]
    hidden = expert_out.shape[2]
    q_span, k_span = HQ * HEAD_SIZE, KEY_VALUE_HEADS * HEAD_SIZE
    group = q_span // n_sp
    head = k_span // n_sp
    segment_ids = segments[0]

    def own(array):
        return lax.dynamic_slice_in_dim(array, sp_index * rows, rows, 0)

    def sum_over(array, axis, count):
        parts = lax.all_to_all(array, axis, split_axis=0, concat_axis=0, tiled=True)
        return jnp.sum(parts.astype(F32), 0)

    small = jnp.concatenate([norm1_gain[:, None], norm2_gain[:, None], router_weight], 1)
    small = jnp.pad(small, ((0, 0), (0, 128 - small.shape[1])))
    pack_width = 2 * group + 128
    any_shape = jax.ShapeDtypeStruct
    tokens_all, late, _, packed, out_mid = wide_call(
        first_kernel,
        "first_gather",
        1,
        (tokens, cotangent, top_idx, qkv_weight, small, out_weight),
        [HBM, VMEM, VMEM, VMEM, VMEM, HBM],
        (
            any_shape((SP, rows, width), BF16),
            any_shape((SP, rows, width + 128), BF16),
            any_shape((SP, weight_rows, pack_width), BF16),
            any_shape((n_fsdp, SP, weight_rows, pack_width), BF16),
            any_shape((SP, weight_rows, width), BF16),
        ),
        [HBM] * 5,
        [pltpu.VMEM((SP, weight_rows, pack_width), BF16), pltpu.VMEM((rows, width + 128), BF16)]
        + [DMA((8,))] * 6
        + [DMA((n_fsdp,))] * 2
        + [DMA((8,))] * 2
        + [DMA((5,))],
    )
    packed = packed.reshape(width, pack_width)
    tokens_all = tokens_all.reshape(seq_len, width)
    late = late.reshape(seq_len, width + 128)
    experts = lax.all_gather(
        jnp.concatenate([expert_in, expert_out], 2), "fsdp", axis=1, tiled=True
    )

    qkv_own = packed[:, : 2 * group]
    small_own = packed[:, 2 * group :]
    small_all = small_own.astype(F32)
    gain_one, gain_two = small_all[:, 0][None, :], small_all[:, 1][None, :]

    hidden_in = tokens_all.astype(F32)
    inverse_one = inverse_rms(hidden_in)
    normed_one = (hidden_in * inverse_one * gain_one).astype(BF16)
    projected = dot(normed_one, qkv_own, ((1,), (0,)))
    cosine, sine = rope_tables(seq_len)
    seg_row, seg_column = segment_ids[None, :], segment_ids[:, None]
    context, query, key2, value2, sums = local_call(
        attention_kernel,
        "attention",
        (projected, cosine, sine, seg_column, seg_row),
        (
            any_shape((seq_len, 128), BF16),
            any_shape((seq_len, 128), BF16),
            any_shape((seq_len, 128), BF16),
            any_shape((seq_len, 128), BF16),
            any_shape((seq_len // BLOCK, 2 * BLOCK, 128), F32),
        ),
        flops=2 * 10**9,
    )
    context_all, out_full = wide_call(
        context_kernel,
        "context_gather",
        2,
        (context, out_mid.reshape(2, SP * weight_rows // 2, width)),
        [HBM] * 2,
        (
            any_shape((seq_len, width), BF16),
            any_shape((n_fsdp, 2, SP * weight_rows // 2, width), BF16),
        ),
        [HBM] * 2,
        [DMA((8,))] * 2 + [DMA((n_fsdp,))] * 4 + [DMA((2,))],
    )
    out_full = out_full.reshape(width, width)
    attended = dot(context_all, out_full, ((1,), (0,)))
    middle = hidden_in + RESIDUAL * attended
    inverse_two = inverse_rms(middle)
    normed_two = (middle * inverse_two * gain_two).astype(BF16)
    n_experts = expert_in.shape[0]
    in_span = expert_in.shape[2]
    mixed, gates, back, grads = wide_call(
        experts_kernel,
        "experts",
        3,
        (normed_two, late, small_own, experts),
        [VMEM, VMEM, VMEM, HBM],
        (
            any_shape((seq_len, width), BF16),
            any_shape((seq_len, 128), F32),
            any_shape((rows, width + 128), F32),
            any_shape((n_fsdp, n_experts, width // n_fsdp, in_span + hidden), BF16),
        ),
        (VMEM, VMEM, VMEM, VMEM),
        [
            pltpu.VMEM((n_experts, width, in_span + hidden), BF16),
            pltpu.VMEM((n_experts, seq_len, hidden), BF16),
            pltpu.VMEM((n_experts, seq_len, in_span), BF16),
            pltpu.VMEM((n_experts, seq_len, width), BF16),
            pltpu.VMEM((SP, rows, width + 128), BF16),
        ]
        + scatter_scratch(rows, width + 128)
        + [DMA((n_experts,))],
    )
    out_own = lax.dynamic_slice_in_dim(out_full, sp_index * group, group, 0)
    share = width // n_fsdp
    shares = group // n_fsdp
    half_grads = (4, share // 2, in_span + hidden)
    half_share = (share // 2, in_span + hidden)
    grad_middle, grad_normed_one, bundle, out_sum, expert_grads, mixed_own = wide_call(
        back_kernel,
        "backward",
        4,
        (
            back, own(gates), own(normed_two), own(middle), cotangent, gain_two, small_own, out_own,
            context, query, key2, value2, sums, cosine, sine, seg_column, seg_row, qkv_own,
            normed_one, grads.reshape(4, 4, n_experts, share, in_span + hidden),
            mixed.reshape(SP, rows, width),
        ),
        [VMEM] * 21,
        (
            any_shape((rows, width), F32),
            any_shape((rows, width), F32),
            any_shape((SP, weight_rows, pack_width), F32),
            any_shape((shares, width), F32),
            any_shape((n_experts, share, in_span + hidden), F32),
            any_shape((rows, width), F32),
        ),
        (VMEM,) * 6,
        [
            pltpu.VMEM((rows, width), BF16),
            pltpu.VMEM((SP, rows, width), BF16),
            pltpu.VMEM((seq_len, group), BF16),
            pltpu.VMEM((seq_len, 2 * group), BF16),
            pltpu.VMEM((seq_len, group), F32),
            pltpu.VMEM((seq_len, group), F32),
            pltpu.VMEM((SP, rows, width), BF16),
            pltpu.VMEM((width, 128), F32),
            pltpu.VMEM((n_fsdp, share, pack_width), BF16),
            pltpu.VMEM((n_fsdp, shares, width), BF16),
            pltpu.VMEM((n_fsdp, share, pack_width), BF16),
            pltpu.VMEM((n_fsdp, shares, width), BF16),
            pltpu.VMEM((SP, weight_rows, pack_width), F32),
            pltpu.VMEM((2,) + half_grads, BF16),
            pltpu.VMEM((2,) + half_grads, BF16),
        ]
        + scatter_scratch(rows, width) * 2
        + quad_scratch(half_grads) * 2
        + quad_scratch(half_share) * 2
        + [DMA((8,))] * 2
        + [DMA((n_fsdp,))] * 4
        + [DMA((8,))] * 2
        + [DMA((4,))],
    )
    block_out = own(middle) + RESIDUAL * mixed_own
    moves = []
    for f in range(n_fsdp):
        for s in range(n_sp):
            moves.append((f * n_sp + s, (s * group + f * shares) // weight_rows))
    if shares == weight_rows:
        out_grad = lax.ppermute(out_sum, ("fsdp", "sp"), moves)
    else:
        whole = lax.all_gather(out_sum, ("fsdp", "sp"), axis=0, tiled=False)
        whole = whole.reshape(n_fsdp, n_sp, shares, width).transpose(1, 0, 2, 3)
        device = lax.axis_index("fsdp") * n_sp + sp_index
        out_grad = lax.dynamic_slice_in_dim(
            whole.reshape(width, width), device * weight_rows, weight_rows, 0
        )

    qkv_grad = jnp.concatenate(
        [
            bundle[:, :, :group].transpose(1, 0, 2).reshape(weight_rows, q_span),
            bundle[:, :, group : group + head].transpose(1, 0, 2).reshape(weight_rows, k_span),
            bundle[:, :, group + head : 2 * group].transpose(1, 0, 2).reshape(weight_rows, k_span),
        ],
        1,
    )
    smalls = jnp.sum(bundle[:, :, 2 * group :], 0)
    gain_two_grad = smalls[:, 1]
    router_grad = smalls[:, 2 : 2 + E]
    gain_one_grad = jnp.sum(qkv_grad * qkv_weight.astype(F32), 1) / norm1_gain.astype(F32)
    hidden_own = tokens.astype(F32)
    input_grad = grad_middle + rms_backward(
        grad_normed_one, hidden_own, inverse_rms(hidden_own), gain_one
    )
    return (
        block_out,
        input_grad,
        gain_one_grad,
        qkv_grad,
        out_grad,
        gain_two_grad,
        router_grad,
        expert_grads[:, :, :in_span],
        expert_grads[:, :, in_span:],
    )


def solution(mesh):
    both = P(("fsdp", "sp"), None)
    flat = P(("fsdp", "sp"))
    expert = P("sp", "fsdp", None)
    return jax.shard_map(
        shards,
        mesh=mesh,
        in_specs=(both, P("fsdp", None), both, both, flat, both, both, flat, both, expert, expert),
        out_specs=(both, both, flat, both, both, flat, both, expert, expert),
        check_vma=False,
    )
```

profile of v0, /device:TPU:1, one launch (start us, length us, event | category | flops | bytes accessed | tf_op | source)
XLA Modules:
  0.0 231.1 jit_solution(11839243785804691875)
XLA Ops:
  7.2 0.0 all-gather.2.cloned.1.call-start
  7.2 1.8 pad_maximum_fusion
  9.0 0.0 all-gather.2.cloned.1.call-update
  9.1 1.4 copy.28.top_idx
  10.5 0.7 copy.26
  11.2 0.7 copy.27
  12.0 0.9 copy.29.seg_column
  12.9 0.0 copy-start
  12.9 1.4 fusion.12.small
  14.2 38.5 %first_gather.1 = (bf16[8,128,1024]{2,1,0:T(8,128)(2,1)}, bf16[8,128,1152]{2,1,0:T(8,128)(2,1)}, bf16[8,8,384]{2,1,0:T(8,128)(2,1)}, bf16[16,8,8,384]{3,2,1,0:T(8,128)(2,1)}, bf16[8,8,1024]{2,1,0:T(8,128)(2,1)}) custom-call(bf16[128,1024]{1,0:T(8,128)(2,1)} %tokens.1, bf16[128,1024]{1,0:T(8,128)(2,1)} %cotangent.3, s32[128,8]{1,0:T(8,128)} %copy.28.top_idx, ...), custom_call_target="tpu_custom_call" | custom-call | flops 20000000000 | bytes 20000000 | tf_op jit(solution)/shard_map/first_gather/pallas_call | solution.py:649
  52.8 0.0 copy-start.9
  52.8 2.0 slice.50.qkv_own
  54.8 1.9 fusion.15
  56.7 0.5 slice_reduce_fusion
  57.2 0.0 copy-start.18
  57.2 0.0 copy-done.9
  57.2 0.5 fusion
  57.7 0.0 copy-done.10
  57.7 0.0 copy-start.1
  57.7 0.0 copy-start.2
  57.7 0.0 copy-start.3
  57.7 0.5 fusion.2.normed_one
  58.3 0.0 copy-start.13
  58.3 1.3 copy-done.13
  59.6 0.0 copy-done.16
  59.6 0.7 fusion.13.proj
  60.3 0.0 copy-done
  60.3 0.0 copy-done.1
  60.3 0.0 copy-done.2
  60.3 0.0 copy-done.3
  60.3 5.3 %attention.1 = (bf16[1024,128]{1,0:T(8,128)(2,1)S(1)}, bf16[1024,128]{1,0:T(8,128)(2,1)S(1)}, bf16[1024,128]{1,0:T(8,128)(2,1)S(1)}, bf16[1024,128]{1,0:T(8,128)(2,1)S(1)}, f32[4,512,128]{2,1,0:T(8,128)S(1)}) custom-call(f32[1024,256]{1,0:T(8,128)S(1)} %fusion.13.proj, f32[1024,128]{1,0:T(8,128)S(1)} %copy-done.2, f32[1024,128]{1,0:T(8,128)S(1)} %copy-done.3, ...), custom_call_target="tpu_custom_call" | custom-call | flops 2000000000 | bytes 2105344 | tf_op jit(solution)/shard_map/attention/pallas_call | solution.py:667
  65.6 0.0 copy-start.4
  65.6 1.1 copy-done.4
  66.7 0.7 copy-done.5
  67.4 0.7 copy-done.6
  68.1 0.7 copy-done.7
  68.8 0.7 copy-done.8
  69.5 26.9 %context_gather.1 = (bf16[1024,1024]{1,0:T(8,128)(2,1)}, bf16[16,2,32,1024]{3,2,1,0:T(8,128)(2,1)}) custom-call(bf16[1024,128]{1,0:T(8,128)(2,1)} %copy-done.5, bf16[2,32,1024]{2,1,0:T(8,128)(2,1)} %bitcast.42), custom_call_target="tpu_custom_call" | custom-call | flops 20000000000 | bytes 20000000 | tf_op jit(solution)/shard_map/context_gather/pallas_call | solution.py:649
  96.4 4.7 %multiply_reduce_fusion = (f32[1024]{0:T(1024)S(1)}, f32[1024,1024]{1,0:T(8,128)S(1)}) fusion(bf16[1024,1024]{1,0:T(8,128)(2,1)} %get-tuple-element.34, bf16[1024,1024]{1,0:T(8,128)(2,1)} %bitcast.34, bf16[8,128,1024]{2,1,0:T(8,128)(2,1)S(1)} %copy-done.10), kind=kOutput, calls=%fused_computation.7 | convolution fusion | flops 2152725504 | bytes 10489856 | tf_op jit(solution)/shard_map/dot_general | solution.py:32
  101.1 0.9 constant_dynamic-slice_fusion.3.middle
  102.1 1.1 copy-done.11
  103.2 0.4 multiply_convert_fusion.normed
  103.7 2.0 constant_dynamic-slice_fusion
  105.6 0.0 copy-done.12
  105.6 41.6 %experts.1 = (bf16[1024,1024]{1,0:T(8,128)(2,1)}, f32[1024,128]{1,0:T(8,128)}, f32[128,1152]{1,0:T(8,128)}, bf16[16,2,64,1536]{3,2,1,0:T(8,128)(2,1)}) custom-call(bf16[1024,1024]{1,0:T(8,128)(2,1)} %copy-done.12, bf16[1024,1152]{1,0:T(8,128)(2,1)} %bitcast.40, bf16[1024,128]{1,0:T(8,128)(2,1)} %get-tuple-element.57.small, ...), custom_call_target="tpu_custom_call" | custom-call | flops 20000000000 | bytes 20000000 | tf_op jit(solution)/shard_map/experts/pallas_call | solution.py:649
  147.2 1.5 constant_dynamic-slice_fusion.2.gates
  148.7 61.4 %backward.1 = (f32[128,1024]{1,0:T(8,128)}, f32[128,1024]{1,0:T(8,128)}, f32[8,8,384]{2,1,0:T(8,128)}, f32[8,1024]{1,0:T(8,128)}, f32[2,64,1536]{2,1,0:T(8,128)}, /*index=5*/f32[128,1024]{1,0:T(8,128)}) custom-call(f32[128,1152]{1,0:T(8,128)} %get-tuple-element.37.back, f32[128,128]{1,0:T(8,128)} %constant_dynamic-slice_fusion.2.gates, ...), custom_call_target="tpu_custom_call" | custom-call | flops 20000000000 | bytes 20000000 | tf_op jit(solution)/shard_map/backward/pallas_call | solution.py:649
  210.1 0.9 slice_bitcast_fusion.1
  211.0 0.8 slice_reduce_fusion.2
  211.8 0.1 reshape.100
  211.9 0.1 reshape.101
  212.0 0.7 multiply_reduce_fusion.1
  212.7 0.0 copy-done.19
  212.7 0.5 convert_divide_fusion
  213.3 1.2 fusion.3
  214.5 2.1 multiply_add_fusion
  216.6 1.9 collective-permute-start
  218.5 2.2 fusion.6
  220.7 0.7 slice_reduce_fusion.3
  221.4 0.8 slice.46
  222.2 0.7 slice.47
  223.0 0.7 slice.45
  223.6 0.0 collective-permute-done
  223.6 0.6 copy.36
  (23 shorter events, 0.1 us)
Async XLA Ops:
  7.2 98.5 %all-gather.2.cloned.1.call-start = ((), (), s32[]{:S(2)}) async-start(), calls=%async_computation | async-start | bytes 6684672 | tf_op jit(solution)/shard_map/all_gather | solution.py:828
  12.9 47.4 %copy-start = (s32[1024,1]{1,0:T(8,128)}, s32[1024,1]{1,0:T(8,128)S(1)}, u32[]{:S(2)}) copy-start(s32[1024,1]{1,0:T(8,128)S(1)} %copy.29.seg_column) | copy-start | bytes 12292
  52.8 4.4 %copy-start.9 = (bf16[8,128,1024]{2,1,0:T(8,128)(2,1)S(1)}, bf16[8,128,1024]{2,1,0:T(8,128)(2,1)}, u32[]{:S(2)}) copy-start(bf16[8,128,1024]{2,1,0:T(8,128)(2,1)} %get-tuple-element.30) | copy-start | bytes 6291460
  54.8 2.9 %copy-start.10 = (bf16[8,128,1024]{2,1,0:T(8,128)(2,1)S(1)}, bf16[8,128,1024]{2,1,0:T(8,128)(2,1)}, u32[]{:S(2)}) copy-start(bf16[8,128,1024]{2,1,0:T(8,128)(2,1)} %get-tuple-element.30) | copy-start | bytes 6291460
  54.8 4.8 %copy-start.16 = (bf16[16,8,8,384]{3,2,1,0:T(8,128)(2,1)S(1)}, bf16[16,8,8,384]{3,2,1,0:T(8,128)(2,1)}, u32[]{:S(2)}) copy-start(bf16[16,8,8,384]{3,2,1,0:T(8,128)(2,1)} %get-tuple-element.31) | copy-start | bytes 2359300
  57.2 44.9 %copy-start.18 = (f32[1024]{0:T(1024)}, f32[1024]{0:T(1024)S(1)}, u32[]{:S(2)}) copy-start(f32[1024]{0:T(1024)S(1)} %get-tuple-element.51) | copy-start | bytes 12292
  57.7 2.6 %copy-start.1 = (s32[1,1024]{1,0:T(1,128)S(1)}, s32[1,1024]{1,0:T(1,128)}, u32[]{:S(2)}) copy-start(s32[1,1024]{1,0:T(1,128)} %seg_row.3) | copy-start | bytes 12292
  57.7 2.6 %copy-start.2 = (f32[1024,128]{1,0:T(8,128)S(1)}, f32[1024,128]{1,0:T(8,128)}, u32[]{:S(2)}) copy-start(f32[1024,128]{1,0:T(8,128)} %constant.31.clone.cosine) | copy-start | bytes 1572868
  57.7 2.6 %copy-start.3 = (f32[1024,128]{1,0:T(8,128)S(1)}, f32[1024,128]{1,0:T(8,128)}, u32[]{:S(2)}) copy-start(f32[1024,128]{1,0:T(8,128)} %constant.32.clone.sine) | copy-start | bytes 1572868
  58.3 1.3 copy-start.13
  65.6 1.1 copy-start.4
  66.7 0.7 copy-start.5
  67.4 0.7 copy-start.6
  68.1 0.7 copy-start.7
  68.8 0.7 copy-start.8
  101.1 2.1 copy-start.11
  103.6 2.0 copy-start.12
  148.7 63.3 %copy-start.17 = (bf16[8,2048]{1,0:T(8,128)(2,1)S(1)}, bf16[8,2048]{1,0:T(8,128)(2,1)}, u32[]{:S(2)}) copy-start(bf16[8,2048]{1,0:T(8,128)(2,1)} %qkv.1) | copy-start | bytes 98308
  148.7 64.0 %copy-start.19 = (bf16[8]{0:T(256)(128)(2,1)S(1)}, bf16[8]{0:T(256)(128)(2,1)}, u32[]{:S(2)}) copy-start(bf16[8]{0:T(256)(128)(2,1)} %param.17) | copy-start | bytes 52
  148.7 64.5 %copy-start.14 = (bf16[128,1024]{1,0:T(8,128)(2,1)S(1)}, bf16[128,1024]{1,0:T(8,128)(2,1)}, u32[]{:S(2)}) copy-start(bf16[128,1024]{1,0:T(8,128)(2,1)} %tokens.1) | copy-start | bytes 786436
  210.1 11.3 %copy-start.15 = (f32[2,64,1536]{2,1,0:T(8,128)S(1)}, f32[2,64,1536]{2,1,0:T(8,128)}, u32[]{:S(2)}) copy-start(f32[2,64,1536]{2,1,0:T(8,128)} %get-tuple-element.50) | copy-start | bytes 2359300
  216.6 7.0 %collective-permute-start = (f32[8,1024]{1,0:T(8,128)}, f32[8,1024]{1,0:T(8,128)S(1)}, u32[]{:S(2)}, u32[]{:S(2)}) collective-permute-start(f32[8,1024]{1,0:T(8,128)} %get-tuple-element.49), channel_id=1, source_target_pairs={{0,0},{1,16},{2,32},{3,48},{4,64},{5,80},{6,96},{7,112},{8,1},{9,1... | collective-permute-start | bytes 98312 | tf_op jit(solution)/shard_map/ppermute | solution.py:955
Sparse Core Ops, SparseCore 0:
  10.1 83.5 all-gather.1
where the time goes:
time: 233 us; the launch traced here: 231 us
  Pallas kernels  174 us (75%)
  local copies, waits for them, and re-layouts  21.7 us (9%)
  between operations  14.3 us (6%)
  other arithmetic  14.1 us (6%)
  matrix products  5.43 us (2%)
    pallas_call x4, Pallas kernels, wide_call(): pl.pallas_call(kernel, name=name, out_shape=outs, in_specs=in_specs, out_...  168 us
    unnamed x42, local copies, waits for them, and re-layouts  8.4 us
    dot_general x2, matrix products, dot(): lax.dot_general(left, right, (contract, ((), ())), preferred_element_type...  5.43 us
    pallas_call x1, Pallas kernels, local_call(): pl.pallas_call(kernel, name=name, out_shape=outs, in_specs=[VMEM] * len(i...  5.25 us
  transfers between devices with their start and end apart: 2, of which 0 were waited for; matrix products, arithmetic and copies ran while one was open for 11% of the time, Pallas kernels for 31%

commit v1 on v0

--- a/solution.py
+++ b/solution.py
@@ -118,13 +118,15 @@
             copy.start()
         self.local.start()
 
-    def finish(self):
+    def forward(self):
         self.first[0].wait_recv()
         for copy in self.next_up:
             copy.start()
         self.first[1].wait_recv()
         for copy in self.next_down:
             copy.start()
+
+    def close(self):
         self.next_up[0].wait_recv()
         self.next_down[0].wait_recv()
         self.last.start()
@@ -133,6 +135,10 @@
             copy.wait_send()
         for copy in (self.first[2], self.next_up[1], self.next_down[1], self.last):
             copy.wait()
+
+    def finish(self):
+        self.forward()
+        self.close()
 
 
 def ring_rows(source, target, send, recv, local):
@@ -164,21 +170,22 @@
     )
 
 
-def spread(axis, size, source, target, send, recv, local, blocks):
+def spread(axis, size, source, target, send, recv, local, blocks, place=None):
     me = lax.axis_index(axis)
+    landing = target.at[me] if place is None else place(me)
     copies = []
     for step in range(1, size):
         peer = lax.rem(me + step, size)
         copies.append(
             remote(
                 source.at[peer] if blocks else source,
-                target.at[me],
+                landing,
                 send.at[step],
                 recv.at[step],
                 **{axis: peer},
             )
         )
-    copies.append(pltpu.make_async_copy(source.at[me] if blocks else source, target.at[me], local))
+    copies.append(pltpu.make_async_copy(source.at[me] if blocks else source, landing, local))
     return copies
 
 
@@ -190,96 +197,6 @@
 def settle(copies):
     for copy in copies:
         copy.wait()
-
-
-def first_kernel(
-    tokens, cotangent, top_idx, qkv, small, outw,
-    tokens_all, late_all, mid, packed_all, out_mid,
-    packed, late, s0, r0, s1, r1, s2, r2, s3, r3, s4, r4, loc,
-):
-    group, q_span = 2 * HEAD_SIZE, HQ * HEAD_SIZE
-    k_span = KEY_VALUE_HEADS * HEAD_SIZE
-    for index in range(SP):
-        k_at = q_span + index * HEAD_SIZE
-        packed[index, :, :group] = qkv[:, index * group : (index + 1) * group]
-        packed[index, :, group : 2 * group] = jnp.concatenate(
-            [
-                qkv[:, k_at : k_at + HEAD_SIZE],
-                qkv[:, k_at + k_span : k_at + k_span + HEAD_SIZE],
-            ],
-            1,
-        )
-        packed[index, :, 2 * group :] = small[...]
-    meet(True)
-    size = lax.axis_size("fsdp")
-    small_copies = spread("sp", SP, packed, mid, s1, r1, loc.at[0], True)
-    run(small_copies)
-    ring = ring_rows(tokens, tokens_all, s0, r0, loc.at[1])
-    ring.start()
-    width = cotangent.shape[1]
-    late[:, :width] = cotangent[...]
-    lane = lax.broadcasted_iota(jnp.int32, (cotangent.shape[0], 128), 1)
-    chosen = jnp.zeros(lane.shape, F32)
-    for choice in range(top_idx.shape[1]):
-        chosen = jnp.where(lane == top_idx[:, choice : choice + 1] + 2, 1.0, chosen)
-    late[:, width:] = chosen.astype(BF16)
-    late_ring = ring_rows(late, late_all, s4, r4, loc.at[4])
-    settle(small_copies)
-    big = spread("fsdp", size, mid, packed_all, s3, r3, loc.at[3], False)
-    run(big)
-    out_copies = spread("sp", SP, outw, out_mid, s2, r2, loc.at[2], False)
-    run(out_copies)
-    late_ring.start()
-    ring.finish()
-    late_ring.finish()
-    settle(out_copies)
-    settle(big)
-
-
-def context_kernel(context, out_mid, context_all, out_all, s0, r0, s1, r1, s2, r2, loc):
-    meet(True)
-    me, core, level, up, down, far = places()
-    size = lax.axis_size("fsdp")
-    mine = lax.axis_index("fsdp")
-    other = level * 2 + (1 - core)
-    keep = pltpu.make_async_copy(out_mid, out_all.at[mine], loc.at[1])
-    keep.start()
-    sent, passed = [], []
-    for step in range(1, size):
-        peer = lax.rem(mine + step, size)
-        sent.append(
-            remote(
-                out_mid.at[core], out_all.at[mine, core], s1.at[step], r1.at[step], fsdp=peer
-            )
-        )
-        source = lax.rem(mine + size - step, size)
-        passed.append(
-            remote(
-                out_all.at[source, core],
-                out_all.at[source, core],
-                s2.at[step],
-                r2.at[step],
-                sp=other,
-            )
-        )
-    ring = ring_columns(context, context_all, s0, r0, loc.at[0])
-    ring.start()
-    run(sent)
-    ring.finish()
-    for copy, onward in zip(sent, passed):
-        copy.wait_recv()
-        onward.start()
-    for copy in sent:
-        copy.wait_send()
-    settle(passed)
-    keep.wait()
-
-
-def gather_kernel(source, target, send, recv, local):
-    meet(False)
-    ring = ring_rows(source, target, send, recv, local)
-    ring.start()
-    ring.finish()
 
 
 class Scatter:
@@ -359,98 +276,6 @@
         DMA((8,)),
         DMA((8,)),
     ]
-
-
-def experts_kernel(
-    normed, late, small, weights,
-    mixed, gates, out, grads,
-    w_buf, acts, grad_acts, grad_results, blocks,
-    other_sums, sums, near, far_parts, send, recv, loads,
-):
-    experts, width, both_span = weights.shape
-    in_span = 2 * both_span // 3
-    hidden = both_span - in_span
-    copies = [
-        pltpu.make_async_copy(weights.at[local], w_buf.at[local], loads.at[local])
-        for local in range(experts)
-    ]
-    run(copies)
-    meet(False)
-    sp_index = lax.axis_index("sp")
-    settle(copies)
-    chunk = 256
-
-    def tokens_block(index, carry):
-        at = pl.ds(pl.multiple_of(index * chunk, chunk), chunk)
-        rows = normed[at, :]
-        logits = dot(rows, small[...], ((1,), (0,)))
-        lane = lax.broadcasted_iota(jnp.int32, logits.shape, 1)
-        shown = jnp.where(late[at, width:].astype(F32) > 0, logits, -jnp.inf)
-        expo = jnp.exp(shown - jnp.max(shown, -1, keepdims=True))
-        gate_rows = expo / jnp.sum(expo, -1, keepdims=True)
-        gates[at, :] = gate_rows
-        grad_mixed = RESIDUAL * late[at, :width].astype(F32)
-        mix = jnp.zeros((chunk, width), F32)
-        back = jnp.zeros((chunk, width), F32)
-        extra = jnp.zeros((chunk, 128), F32)
-        for local in range(experts):
-            expert = lane == sp_index * experts + local + 2
-            gate = jnp.sum(jnp.where(expert, gate_rows, 0.0), -1, keepdims=True)
-            pre_act = dot(rows, w_buf[local, :, :in_span], ((1,), (0,)))
-            gate_part, up_part = pre_act[:, :hidden], pre_act[:, hidden:]
-            sigmoid = 1.0 / (1.0 + jnp.exp(-gate_part))
-            silu = gate_part * sigmoid
-            act = (silu * up_part).astype(BF16)
-            acts[local, at, :] = act
-            produced = dot(act, w_buf[local, :, in_span:], ((1,), (1,))).astype(BF16).astype(F32)
-            mix = mix + gate * produced
-            grad_gate = jnp.sum(grad_mixed * produced, -1, keepdims=True)
-            extra = extra + jnp.where(expert, gate * grad_gate, 0.0)
-            grad_result = (gate * grad_mixed).astype(BF16)
-            grad_results[local, at, :] = grad_result
-            grad_act = dot(grad_result, w_buf[local, :, in_span:], ((1,), (0,)))
-            grad_gate_part = grad_act * up_part * sigmoid * (1.0 + gate_part * (1.0 - sigmoid))
-            grad_pre = jnp.concatenate([grad_gate_part, grad_act * silu], 1).astype(BF16)
-            grad_acts[local, at, :] = grad_pre
-            back = back + dot(grad_pre, w_buf[local, :, :in_span], ((1,), (1,)))
-        mixed[at, :] = mix.astype(BF16)
-        per_block = blocks.shape[1]
-        count = chunk // per_block
-        for piece in range(count):
-            place = slice(piece * per_block, (piece + 1) * per_block)
-            blocks[index * count + piece, :, :width] = back[place].astype(BF16)
-            blocks[index * count + piece, :, width:] = extra[place].astype(BF16)
-        return carry
-
-    lax.fori_loop(0, normed.shape[0] // chunk, tokens_block, 0)
-    scatter = Scatter(blocks, other_sums, sums, near, far_parts, send, recv)
-    scatter.start()
-    owners = grads.shape[0]
-    share = width // owners
-    tile = 256
-    count = tile // share
-
-    def weight_tile(index, carry):
-        columns = pl.ds(pl.multiple_of(index * tile, tile), tile)
-        turned = normed[:, columns]
-        for local in range(experts):
-            value = dot(turned, grad_acts[local], ((0,), (0,))).astype(BF16)
-            grads[pl.ds(index * count, count), local, :, :in_span] = value.reshape(
-                count, share, in_span
-            )
-            value = dot(grad_results[local, :, columns], acts[local], ((0,), (0,))).astype(BF16)
-            grads[pl.ds(index * count, count), local, :, in_span:] = value.reshape(
-                count, share, hidden
-            )
-        return carry
-
-    tiles = width // tile
-    lax.fori_loop(0, tiles // 4, weight_tile, 0)
-    scatter.middle()
-    lax.fori_loop(tiles // 4, tiles // 2, weight_tile, 0)
-    scatter.near_blocks()
-    lax.fori_loop(tiles // 2, tiles, weight_tile, 0)
-    scatter.end(out)
 
 
 class Quad:
@@ -645,37 +470,6 @@
     settle(shares)
 
 
-def wide_call(kernel, name, number, inputs, in_specs, outs, out_specs, scratch):
-    return pl.pallas_call(
-        kernel,
-        name=name,
-        out_shape=outs,
-        in_specs=in_specs,
-        out_specs=out_specs,
-        scratch_shapes=scratch,
-        cost_estimate=pl.CostEstimate(
-            flops=2 * 10**10, bytes_accessed=2 * 10**7, transcendentals=0
-        ),
-        compiler_params=pltpu.CompilerParams(
-            collective_id=number, has_side_effects=True, vmem_limit_bytes=56 * 2**20
-        ),
-    )(*inputs)
-
-
-def local_call(kernel, name, inputs, outs, scratch=(), flops=0):
-    moved = sum(array.size * array.dtype.itemsize for array in inputs)
-    return pl.pallas_call(
-        kernel,
-        name=name,
-        out_shape=outs,
-        in_specs=[VMEM] * len(inputs),
-        out_specs=jax.tree.map(lambda _: VMEM, outs),
-        scratch_shapes=scratch,
-        cost_estimate=pl.CostEstimate(flops=flops, bytes_accessed=moved, transcendentals=0),
-        compiler_params=pltpu.CompilerParams(vmem_limit_bytes=48 * 2**20),
-    )(*inputs)
-
-
 def swap_halves(value):
     wide = value.shape[-1]
     lane = lax.broadcasted_iota(jnp.int32, value.shape, 1)
@@ -766,6 +560,334 @@
     grad_proj[:, 128:] = jnp.where(is_first, moved, other).astype(BF16)
 
 
+class QuadGather:
+    def __init__(self, axis, block, part, send, recv):
+        mine = lax.axis_index("fsdp")
+        y, x = mine // 4, lax.rem(mine, 4)
+        here = x if axis == "x" else y
+        up, down = lax.rem(here + 1, 4), lax.rem(here + 3, 4)
+
+        def go(ref, number, place):
+            device = y * 4 + place if axis == "x" else place * 4 + x
+            return remote(ref, ref, send.at[number], recv.at[number], fsdp=device)
+
+        self.own = [go(block(here), 0, up), go(block(here), 1, down)]
+        self.onward = [go(part(down, 0), 2, up), go(part(up, 1), 3, down)]
+
+    def start(self):
+        run(self.own)
+
+    def forward(self):
+        for came, onward in zip(self.own, self.onward):
+            came.wait_recv()
+            onward.start()
+
+    def close(self):
+        for copy in self.onward:
+            copy.wait_recv()
+        for copy in self.own + self.onward:
+            copy.wait_send()
+
+
+def forward_kernel(
+    tokens, cotangent, top_idx, qkv, small, outw, expert_in, expert_out,
+    cosine, sine, seg_column, seg_row,
+    mid, out_mid, qkv_own, small_own, gains, normed_one, context, query, key2, value2, sums,
+    out_own, normed_own, middle_own, gates_own, mixed, back, grads,
+    packed, late, tokens_all, late_all, packed_all, out_all, w_buf, context_all, proj, normed,
+    acts, grad_acts, grad_results, blocks, middle_part, gates,
+    *scratch,
+):
+    scratch = list(scratch)
+
+    def take(count):
+        taken = scratch[:count]
+        del scratch[:count]
+        return taken
+
+    scatter_parts = take(6)
+    (s0, r0, s1, r1, s2, r2, s3, r3, s4, r4, s5, r5, s6, r6, s7, r7, loc) = take(17)
+    quad_sems = take(8)
+    group, q_span = 2 * HEAD_SIZE, HQ * HEAD_SIZE
+    k_span = KEY_VALUE_HEADS * HEAD_SIZE
+    me, core, level, up, down, far = places()
+    size = lax.axis_size("fsdp")
+    mine = lax.axis_index("fsdp")
+    y, x = mine // 4, lax.rem(mine, 4)
+    other = level * 2 + (1 - core)
+    experts = expert_in.shape[0]
+    in_span, hidden = expert_in.shape[2], expert_out.shape[2]
+    rows, width = cotangent.shape
+    seq_len = normed.shape[0]
+    chunk = 256
+    per_chunk = chunk // rows
+
+    shard_copies = []
+    for local in range(experts):
+        shard_copies += [
+            pltpu.make_async_copy(
+                expert_in.at[local], w_buf.at[local, y, x, :, pl.ds(0, in_span)], loc.at[6 + local]
+            ),
+            pltpu.make_async_copy(
+                expert_out.at[local],
+                w_buf.at[local, y, x, :, pl.ds(in_span, hidden)],
+                loc.at[8 + local],
+            ),
+        ]
+    run(shard_copies)
+    for index in range(SP):
+        k_at = q_span + index * HEAD_SIZE
+        packed[index, :, :group] = qkv[:, index * group : (index + 1) * group]
+        packed[index, :, group : 2 * group] = jnp.concatenate(
+            [
+                qkv[:, k_at : k_at + HEAD_SIZE],
+                qkv[:, k_at + k_span : k_at + k_span + HEAD_SIZE],
+            ],
+            1,
+        )
+        packed[index, :, 2 * group :] = small[...]
+    own_rows = packed.shape[1]
+
+    def rows_of(target):
+        return lambda index: target.at[pl.ds(pl.multiple_of(index * own_rows, own_rows), own_rows)]
+
+    meet(True)
+    small_copies = spread("sp", SP, packed, mid, s1, r1, loc.at[0], True, rows_of(mid))
+    run(small_copies)
+    ring = ring_rows(tokens, tokens_all, s0, r0, loc.at[1])
+    ring.start()
+    out_copies = spread("sp", SP, outw, out_mid, s2, r2, loc.at[2], False, rows_of(out_mid))
+    run(out_copies)
+    late[:, :width] = cotangent[...]
+    lane = lax.broadcasted_iota(jnp.int32, (rows, 128), 1)
+    chosen = jnp.zeros(lane.shape, F32)
+    for choice in range(top_idx.shape[1]):
+        chosen = jnp.where(lane == top_idx[:, choice : choice + 1] + 2, 1.0, chosen)
+    late[:, width:] = chosen.astype(BF16)
+    settle(small_copies)
+    big = spread("fsdp", size, mid, packed_all, s3, r3, loc.at[3], False)
+    run(big)
+    ring.forward()
+    late_ring = ring_rows(late, late_all, s4, r4, loc.at[4])
+    late_ring.start()
+    settle(shard_copies)
+    first = [
+        QuadGather(
+            "x",
+            lambda index: w_buf.at[0, y, index],
+            lambda index, side: w_buf.at[0, y, index, pl.ds(side * 32, 32)],
+            *quad_sems[0:2],
+        ),
+        QuadGather(
+            "y",
+            lambda index: w_buf.at[1, index, x],
+            lambda index, side: w_buf.at[1, index, x, pl.ds(side * 32, 32)],
+            *quad_sems[2:4],
+        ),
+    ]
+    second = [
+        QuadGather(
+            "y",
+            lambda index: w_buf.at[0, index],
+            lambda index, side: w_buf.at[0, index, pl.ds(side * 2, 2)],
+            *quad_sems[4:6],
+        ),
+        QuadGather(
+            "x",
+            lambda index: w_buf.at[1, :, index],
+            lambda index, side: w_buf.at[1, pl.ds(side * 2, 2), index],
+            *quad_sems[6:8],
+        ),
+    ]
+    ring.close()
+    settle(big)
+    for quad in first:
+        quad.start()
+    settle(out_copies)
+    half_rows = out_all.shape[2]
+    own_half = out_mid.at[pl.ds(pl.multiple_of(core * half_rows, half_rows), half_rows)]
+    keep = [
+        pltpu.make_async_copy(
+            out_mid.at[pl.ds(side * half_rows, half_rows)],
+            out_all.at[mine, side],
+            loc.at[10 + side],
+        )
+        for side in range(2)
+    ]
+    run(keep)
+    sent, passed = [], []
+    for step in range(1, size):
+        peer = lax.rem(mine + step, size)
+        sent.append(
+            remote(own_half, out_all.at[mine, core], s5.at[step], r5.at[step], fsdp=peer)
+        )
+        source = lax.rem(mine + size - step, size)
+        passed.append(
+            remote(
+                out_all.at[source, core],
+                out_all.at[source, core],
+                s6.at[step],
+                r6.at[step],
+                sp=other,
+            )
+        )
+    run(sent)
+    everything = packed_all[...].reshape(width, packed_all.shape[2])
+    qkv_own[...] = everything[:, : 2 * group]
+    small_own[...] = everything[:, 2 * group :]
+    pick = (
+        lax.broadcasted_iota(jnp.int32, (8, 128), 0) == lax.broadcasted_iota(jnp.int32, (8, 128), 1)
+    ).astype(F32).astype(BF16)
+    gains[...] = dot(pick, small_own[...], ((1,), (1,)))
+
+    def first_norm(index, carry):
+        at = pl.ds(pl.multiple_of(index * chunk, chunk), chunk)
+        value = tokens_all[pl.ds(index * per_chunk, per_chunk)].reshape(chunk, width).astype(F32)
+        normal = (value * inverse_rms(value) * gains[0:1, :]).astype(BF16)
+        normed_one[at, :] = normal
+        proj[at, :] = dot(normal, qkv_own[...], ((1,), (0,)))
+        return carry
+
+    lax.fori_loop(0, seq_len // chunk, first_norm, 0)
+    for quad in first:
+        quad.forward()
+    late_ring.forward()
+    attention_kernel(
+        proj, cosine, sine, seg_column, seg_row, context, query, key2, value2, sums
+    )
+    context_ring = ring_columns(context, context_all, s7, r7, loc.at[5])
+    context_ring.start()
+    for quad in first:
+        quad.close()
+    for quad in second:
+        quad.start()
+    late_ring.close()
+    for copy, onward in zip(sent, passed):
+        copy.wait_recv()
+        onward.start()
+    context_ring.forward()
+    context_ring.close()
+    for copy in sent:
+        copy.wait_send()
+    settle(passed)
+    settle(keep)
+    out_own[...] = out_all[pl.ds(2 * me, 2)].reshape(out_own.shape)
+
+    def second_norm(index, carry):
+        at = pl.ds(pl.multiple_of(index * chunk, chunk), chunk)
+        value = tokens_all[pl.ds(index * per_chunk, per_chunk)].reshape(chunk, width).astype(F32)
+        out_full = out_all[...].reshape(width, width)
+        value = value + RESIDUAL * dot(context_all[at, :], out_full, ((1,), (0,)))
+
+        @pl.when(index == me // per_chunk)
+        def _():
+            middle_part[...] = value.reshape(middle_part.shape)
+
+        normed[at, :] = (value * inverse_rms(value) * gains[1:2, :]).astype(BF16)
+        return carry
+
+    lax.fori_loop(0, seq_len // chunk, second_norm, 0)
+    for quad in second:
+        quad.forward()
+    middle_own[...] = middle_part[lax.rem(me, per_chunk)]
+    at_own = pl.ds(pl.multiple_of(me * rows, rows), rows)
+    normed_own[...] = normed[at_own, :]
+    for quad in second:
+        quad.close()
+
+    def weights_of(local, low, high):
+        return w_buf[local, :, :, :, low:high].reshape(width, high - low)
+
+    def tokens_block(index, carry):
+        at = pl.ds(pl.multiple_of(index * chunk, chunk), chunk)
+        rows_in = normed[at, :]
+        logits = dot(rows_in, small_own[...], ((1,), (0,)))
+        late_rows = late_all[pl.ds(index * per_chunk, per_chunk)].reshape(chunk, width + 128)
+        lanes = lax.broadcasted_iota(jnp.int32, logits.shape, 1)
+        shown = jnp.where(late_rows[:, width:].astype(F32) > 0, logits, -jnp.inf)
+        expo = jnp.exp(shown - jnp.max(shown, -1, keepdims=True))
+        gate_rows = expo / jnp.sum(expo, -1, keepdims=True)
+        gates[at, :] = gate_rows
+        grad_mixed = RESIDUAL * late_rows[:, :width].astype(F32)
+        mix = jnp.zeros((chunk, width), F32)
+        grad_rows = jnp.zeros((chunk, width), F32)
+        extra = jnp.zeros((chunk, 128), F32)
+        for local in range(experts):
+            expert = lanes == me * experts + local + 2
+            gate = jnp.sum(jnp.where(expert, gate_rows, 0.0), -1, keepdims=True)
+            pre_act = dot(rows_in, weights_of(local, 0, in_span), ((1,), (0,)))
+            gate_part, up_part = pre_act[:, :hidden], pre_act[:, hidden:]
+            sigmoid = 1.0 / (1.0 + jnp.exp(-gate_part))
+            silu = gate_part * sigmoid
+            act = (silu * up_part).astype(BF16)
+            acts[local, at, :] = act
+            w_out = weights_of(local, in_span, in_span + hidden)
+            produced = dot(act, w_out, ((1,), (1,))).astype(BF16).astype(F32)
+            mix = mix + gate * produced
+            grad_gate = jnp.sum(grad_mixed * produced, -1, keepdims=True)
+            extra = extra + jnp.where(expert, gate * grad_gate, 0.0)
+            grad_result = (gate * grad_mixed).astype(BF16)
+            grad_results[local, at, :] = grad_result
+            grad_act = dot(grad_result, w_out, ((1,), (0,)))
+            grad_gate_part = grad_act * up_part * sigmoid * (1.0 + gate_part * (1.0 - sigmoid))
+            grad_pre = jnp.concatenate([grad_gate_part, grad_act * silu], 1).astype(BF16)
+            grad_acts[local, at, :] = grad_pre
+            grad_rows = grad_rows + dot(grad_pre, weights_of(local, 0, in_span), ((1,), (1,)))
+        mixed[at, :] = mix.astype(BF16)
+        for piece in range(per_chunk):
+            place = slice(piece * rows, (piece + 1) * rows)
+            blocks[index * per_chunk + piece, :, :width] = grad_rows[place].astype(BF16)
+            blocks[index * per_chunk + piece, :, width:] = extra[place].astype(BF16)
+        return carry
+
+    lax.fori_loop(0, seq_len // chunk, tokens_block, 0)
+    scatter = Scatter(blocks, *scatter_parts)
+    scatter.start()
+    gates_own[...] = gates[at_own, :]
+    owners = grads.shape[0]
+    share = width // owners
+    count = chunk // share
+
+    def weight_tile(index, carry):
+        columns = pl.ds(pl.multiple_of(index * chunk, chunk), chunk)
+        turned = normed[:, columns]
+        for local in range(experts):
+            value = dot(turned, grad_acts[local], ((0,), (0,))).astype(BF16)
+            grads[pl.ds(index * count, count), local, :, :in_span] = value.reshape(
+                count, share, in_span
+            )
+            value = dot(grad_results[local, :, columns], acts[local], ((0,), (0,))).astype(BF16)
+            grads[pl.ds(index * count, count), local, :, in_span:] = value.reshape(
+                count, share, hidden
+            )
+        return carry
+
+    tiles = width // chunk
+    lax.fori_loop(0, tiles // 4, weight_tile, 0)
+    scatter.middle()
+    lax.fori_loop(tiles // 4, tiles // 2, weight_tile, 0)
+    scatter.near_blocks()
+    lax.fori_loop(tiles // 2, tiles, weight_tile, 0)
+    scatter.end(back)
+
+
+def wide_call(kernel, name, number, inputs, in_specs, outs, out_specs, scratch):
+    return pl.pallas_call(
+        kernel,
+        name=name,
+        out_shape=outs,
+        in_specs=in_specs,
+        out_specs=out_specs,
+        scratch_shapes=scratch,
+        cost_estimate=pl.CostEstimate(
+            flops=2 * 10**10, bytes_accessed=2 * 10**7, transcendentals=0
+        ),
+        compiler_params=pltpu.CompilerParams(
+            collective_id=number, has_side_effects=True, vmem_limit_bytes=60 * 2**20
+        ),
+    )(*inputs)
+
+
 def shards(
     tokens,
     segments,
@@ -789,114 +911,73 @@
     q_span, k_span = HQ * HEAD_SIZE, KEY_VALUE_HEADS * HEAD_SIZE
     group = q_span // n_sp
     head = k_span // n_sp
-    segment_ids = segments[0]
-
-    def own(array):
-        return lax.dynamic_slice_in_dim(array, sp_index * rows, rows, 0)
-
-    def sum_over(array, axis, count):
-        parts = lax.all_to_all(array, axis, split_axis=0, concat_axis=0, tiled=True)
-        return jnp.sum(parts.astype(F32), 0)
-
     small = jnp.concatenate([norm1_gain[:, None], norm2_gain[:, None], router_weight], 1)
     small = jnp.pad(small, ((0, 0), (0, 128 - small.shape[1])))
     pack_width = 2 * group + 128
     any_shape = jax.ShapeDtypeStruct
-    tokens_all, late, _, packed, out_mid = wide_call(
-        first_kernel,
-        "first_gather",
-        1,
-        (tokens, cotangent, top_idx, qkv_weight, small, out_weight),
-        [HBM, VMEM, VMEM, VMEM, VMEM, HBM],
-        (
-            any_shape((SP, rows, width), BF16),
-            any_shape((SP, rows, width + 128), BF16),
-            any_shape((SP, weight_rows, pack_width), BF16),
-            any_shape((n_fsdp, SP, weight_rows, pack_width), BF16),
-            any_shape((SP, weight_rows, width), BF16),
-        ),
-        [HBM] * 5,
-        [pltpu.VMEM((SP, weight_rows, pack_width), BF16), pltpu.VMEM((rows, width + 128), BF16)]
-        + [DMA((8,))] * 6
-        + [DMA((n_fsdp,))] * 2
-        + [DMA((8,))] * 2
-        + [DMA((5,))],
-    )
-    packed = packed.reshape(width, pack_width)
-    tokens_all = tokens_all.reshape(seq_len, width)
-    late = late.reshape(seq_len, width + 128)
-    experts = lax.all_gather(
-        jnp.concatenate([expert_in, expert_out], 2), "fsdp", axis=1, tiled=True
-    )
-
-    qkv_own = packed[:, : 2 * group]
-    small_own = packed[:, 2 * group :]
-    small_all = small_own.astype(F32)
-    gain_one, gain_two = small_all[:, 0][None, :], small_all[:, 1][None, :]
-
-    hidden_in = tokens_all.astype(F32)
-    inverse_one = inverse_rms(hidden_in)
-    normed_one = (hidden_in * inverse_one * gain_one).astype(BF16)
-    projected = dot(normed_one, qkv_own, ((1,), (0,)))
     cosine, sine = rope_tables(seq_len)
-    seg_row, seg_column = segment_ids[None, :], segment_ids[:, None]
-    context, query, key2, value2, sums = local_call(
-        attention_kernel,
-        "attention",
-        (projected, cosine, sine, seg_column, seg_row),
-        (
-            any_shape((seq_len, 128), BF16),
-            any_shape((seq_len, 128), BF16),
-            any_shape((seq_len, 128), BF16),
-            any_shape((seq_len, 128), BF16),
-            any_shape((seq_len // BLOCK, 2 * BLOCK, 128), F32),
-        ),
-        flops=2 * 10**9,
-    )
-    context_all, out_full = wide_call(
-        context_kernel,
-        "context_gather",
-        2,
-        (context, out_mid.reshape(2, SP * weight_rows // 2, width)),
-        [HBM] * 2,
-        (
-            any_shape((seq_len, width), BF16),
-            any_shape((n_fsdp, 2, SP * weight_rows // 2, width), BF16),
-        ),
-        [HBM] * 2,
-        [DMA((8,))] * 2 + [DMA((n_fsdp,))] * 4 + [DMA((2,))],
-    )
-    out_full = out_full.reshape(width, width)
-    attended = dot(context_all, out_full, ((1,), (0,)))
-    middle = hidden_in + RESIDUAL * attended
-    inverse_two = inverse_rms(middle)
-    normed_two = (middle * inverse_two * gain_two).astype(BF16)
+    seg_row, seg_column = segments, segments.reshape(seq_len, 1)
     n_experts = expert_in.shape[0]
     in_span = expert_in.shape[2]
-    mixed, gates, back, grads = wide_call(
-        experts_kernel,
-        "experts",
-        3,
-        (normed_two, late, small_own, experts),
-        [VMEM, VMEM, VMEM, HBM],
+    slab = any_shape((seq_len, group), BF16)
+    (
+        _, _, qkv_own, small_own, gains, normed_one, context, query, key2, value2, sums,
+        out_own, normed_own, middle_own, gates_own, mixed, back, grads,
+    ) = wide_call(
+        forward_kernel,
+        "forward",
+        1,
         (
+            tokens, cotangent, top_idx, qkv_weight, small, out_weight, expert_in, expert_out,
+            cosine, sine, seg_column, seg_row,
+        ),
+        [HBM] + [VMEM] * 4 + [HBM] * 3 + [VMEM] * 4,
+        (
+            any_shape((SP * weight_rows, pack_width), BF16),
+            any_shape((SP * weight_rows, width), BF16),
+            any_shape((width, 2 * group), BF16),
+            any_shape((width, 128), BF16),
+            any_shape((8, width), F32),
             any_shape((seq_len, width), BF16),
-            any_shape((seq_len, 128), F32),
+            slab, slab, slab, slab,
+            any_shape((seq_len // BLOCK, 2 * BLOCK, 128), F32),
+            any_shape((group, width), BF16),
+            any_shape((rows, width), BF16),
+            any_shape((rows, width), F32),
+            any_shape((rows, 128), F32),
+            any_shape((seq_len, width), BF16),
             any_shape((rows, width + 128), F32),
             any_shape((n_fsdp, n_experts, width // n_fsdp, in_span + hidden), BF16),
         ),
-        (VMEM, VMEM, VMEM, VMEM),
+        (HBM, HBM) + (VMEM,) * 16,
         [
-            pltpu.VMEM((n_experts, width, in_span + hidden), BF16),
+            pltpu.VMEM((SP, weight_rows, pack_width), BF16),
+            pltpu.VMEM((rows, width + 128), BF16),
+            pltpu.VMEM((SP, rows, width), BF16),
+            pltpu.VMEM((SP, rows, width + 128), BF16),
+            pltpu.VMEM((n_fsdp, SP * weight_rows, pack_width), BF16),
+            pltpu.VMEM((n_fsdp, 2, SP * weight_rows // 2, width), BF16),
+            pltpu.VMEM((n_experts, 4, 4, width // n_fsdp, in_span + hidden), BF16),
+            pltpu.VMEM((seq_len, width), BF16),
+            pltpu.VMEM((seq_len, 2 * group), F32),
+            pltpu.VMEM((seq_len, width), BF16),
             pltpu.VMEM((n_experts, seq_len, hidden), BF16),
             pltpu.VMEM((n_experts, seq_len, in_span), BF16),
             pltpu.VMEM((n_experts, seq_len, width), BF16),
             pltpu.VMEM((SP, rows, width + 128), BF16),
+            pltpu.VMEM((2, rows, width), F32),
+            pltpu.VMEM((seq_len, 128), F32),
         ]
         + scatter_scratch(rows, width + 128)
-        + [DMA((n_experts,))],
-    )
-    out_own = lax.dynamic_slice_in_dim(out_full, sp_index * group, group, 0)
+        + [DMA((8,))] * 6
+        + [DMA((n_fsdp,))] * 2
+        + [DMA((8,))] * 2
+        + [DMA((n_fsdp,))] * 4
+        + [DMA((8,))] * 2
+        + [DMA((12,))]
+        + [DMA((4,))] * 8,
+    )
+    gain_one, gain_two = gains[0:1], gains[1:2]
     share = width // n_fsdp
     shares = group // n_fsdp
     half_grads = (4, share // 2, in_span + hidden)
@@ -906,7 +987,7 @@
         "backward",
         4,
         (
-            back, own(gates), own(normed_two), own(middle), cotangent, gain_two, small_own, out_own,
+            back, gates_own, normed_own, middle_own, cotangent, gain_two, small_own, out_own,
             context, query, key2, value2, sums, cosine, sine, seg_column, seg_row, qkv_own,
             normed_one, grads.reshape(4, 4, n_experts, share, in_span + hidden),
             mixed.reshape(SP, rows, width),
@@ -946,7 +1027,7 @@
         + [DMA((8,))] * 2
         + [DMA((4,))],
     )
-    block_out = own(middle) + RESIDUAL * mixed_own
+    block_out = middle_own + RESIDUAL * mixed_own
     moves = []
     for f in range(n_fsdp):
         for s in range(n_sp):

time: 233 us -> 202 us (0.87)
  between operations: 14.3 us -> 0.72 us
  local copies, waits for them, and re-layouts: 21.7 us -> 10.6 us
  other arithmetic: 14.1 us -> 7.23 us
  Pallas kernels: 174 us -> 180 us
  matrix products: 5.43 us -> 0 us
    pallas_call x4 -> x2, Pallas kernels: 168 us -> 180 us  [wide_call(): pl.pallas_call(kernel, name=name, out_shape=outs, in_specs=in_specs, out_...]
    unnamed x42 -> x12, local copies, waits for them, and re-layouts: 8.4 us -> 2.05 us
    dot_general x2 -> x0, matrix products: 5.43 us -> none  [dot(): lax.dot_general(left, right, (contract, ((), ())), preferred_element_type...]
    pallas_call x1 -> x0, Pallas kernels: 5.25 us -> none  [local_call(): pl.pallas_call(kernel, name=name, out_shape=outs, in_specs=[VMEM] * len(i...]
    dynamic_slice x3 -> x0, local copies, waits for them, and re-layouts: 4.39 us -> none  [the longest x2 2.4 us: own(): return lax.dynamic_slice_in_dim(array, sp_index * rows, rows, 0)]
  transfers between devices with their start and end apart: 2 -> 1, of which waited for: 0 -> 0; matrix products, arithmetic and copies ran while one was open for 11% -> 5% of each run, Pallas kernels for 31% -> 0%
where the time goes in v1:
time: 202 us; the launch traced here: 201 us
  Pallas kernels  180 us (89%)
  local copies, waits for them, and re-layouts  10.6 us (5%)
  other arithmetic  7.23 us (4%)
  starting transfers between devices  3.17 us (2%)
    pallas_call x2, Pallas kernels, wide_call(): pl.pallas_call(kernel, name=name, out_shape=outs, in_specs=in_specs, out_...  180 us
  transfers between devices with their start and end apart: 1, of which 0 were waited for; matrix products, arithmetic and copies ran while one was open for 5% of the time, Pallas kernels for 0%

profile of v1, /device:TPU:1, one launch (start us, length us, event | category | flops | bytes accessed | tf_op | source)
XLA Modules:
  0.0 201.3 jit_solution(4360784474955783143)
XLA Ops:
  0.6 0.7 copy.26
  1.4 0.7 copy.25
  2.1 1.4 copy.27.top_idx
  3.5 1.7 copy.28.seg_column
  5.2 1.3 fusion.9.small
  6.6 114.8 %forward.1 = (bf16[64,384]{1,0:T(8,128)(2,1)}, bf16[64,1024]{1,0:T(8,128)(2,1)}, bf16[1024,256]{1,0:T(8,128)(2,1)}, bf16[1024,128]{1,0:T(8,128)(2,1)}, f32[8,102...) custom-call(bf16[128,1024]{1,0:T(8,128)(2,1)} %tokens.1, ...), custom_call_target="tpu_custom_call" | custom-call | flops 20000000000 | bytes 20000000 | tf_op jit(solution)/shard_map/forward/pallas_call | solution.py:875
  121.4 1.4 fusion.10
  122.9 0.0 copy-start
  122.9 0.0 copy-start.3
  122.9 0.0 copy-start.4
  122.9 0.0 copy-start.2
  122.9 64.7 %backward.1 = (f32[128,1024]{1,0:T(8,128)}, f32[128,1024]{1,0:T(8,128)}, f32[8,8,384]{2,1,0:T(8,128)}, f32[8,1024]{1,0:T(8,128)}, f32[2,64,1536]{2,1,0:T(8,128)}, /*index=5*/f32[128,1024]{1,0:T(8,128)}) custom-call(f32[128,1152]{1,0:T(8,128)} %get-tuple-element.32.back, f32[128,128]{1,0:T(8,128)} %get-tuple-element.33.gates, ...), custom_call_target="tpu_custom_call" | custom-call | flops 20000000000 | bytes 20000000 | tf_op jit(solution)/shard_map/backward/pallas_call | solution.py:875
  187.6 3.2 %collective-permute-start = (f32[8,1024]{1,0:T(8,128)}, f32[8,1024]{1,0:T(8,128)S(1)}, u32[]{:S(2)}, u32[]{:S(2)}) collective-permute-start(f32[8,1024]{1,0:T(8,128)} %get-tuple-element.51), channel_id=1, source_target_pairs={{0,0},{1,16},{2,32},{3,48},{4,64},{5,80},{6,96},{7,112},{8,1},{9,1... | collective-permute-start | bytes 98312 | tf_op jit(solution)/shard_map/ppermute | solution.py:1036
  190.8 0.8 slice_reduce_fusion
  191.6 0.9 slice_bitcast_fusion.1
  192.5 0.0 copy-done
  192.5 1.2 fusion
  193.7 0.0 copy-start.1
  193.8 0.1 reshape.58
  193.9 0.1 reshape.59
  193.9 0.0 copy-done.3
  193.9 0.7 multiply_reduce_fusion
  194.7 0.0 copy-done.4
  194.7 0.5 convert_divide_fusion
  195.2 0.0 copy-done.2
  195.2 2.6 %fusion.3 = (f32[128,1024]{1,0:T(8,128)}, f32[128,1024]{1,0:T(8,128)}) fusion(f32[128,1024]{1,0:T(8,128)} %get-tuple-element.48, bf16[128,1024]{1,0:T(8,128)(2,1)S(1)} %copy-done, f32[128,1024]{1,0:T(8,128)} %get-tuple-element.49, f32[128]{0:T(128)S(1)} %broadcast_multiply_fusion, f32[128]{0:T(128)S(1)} %get-tuple-element.64, f32[1024]{0:T(1024)S(1)} %bitcast.15, ...), kind=kLoop, calls=%fused_computation.6 | loop fusion | flops 1179648 | bytes 3413504 | tf_op jit(solution)/shard_map/add | solution.py:1058
  197.8 0.7 slice_reduce_fusion.1
  198.5 0.7 slice.37
  199.2 0.0 copy-done.1
  199.2 0.7 slice.39
  199.9 0.8 slice.38
  200.7 0.0 collective-permute-done
  200.7 0.6 copy.33
  (4 shorter events, 0.0 us)
Async XLA Ops:
  122.9 69.6 %copy-start = (bf16[128,1024]{1,0:T(8,128)(2,1)S(1)}, bf16[128,1024]{1,0:T(8,128)(2,1)}, u32[]{:S(2)}) copy-start(bf16[128,1024]{1,0:T(8,128)(2,1)} %tokens.1) | copy-start | bytes 786436
  122.9 71.1 %copy-start.3 = (bf16[8,2048]{1,0:T(8,128)(2,1)S(1)}, bf16[8,2048]{1,0:T(8,128)(2,1)}, u32[]{:S(2)}) copy-start(bf16[8,2048]{1,0:T(8,128)(2,1)} %qkv.1) | copy-start | bytes 98308
  122.9 71.8 %copy-start.4 = (bf16[8]{0:T(256)(128)(2,1)S(1)}, bf16[8]{0:T(256)(128)(2,1)}, u32[]{:S(2)}) copy-start(bf16[8]{0:T(256)(128)(2,1)} %param.17) | copy-start | bytes 52
  122.9 72.4 %copy-start.2 = (f32[128,1024]{1,0:T(8,128)S(1)}, f32[128,1024]{1,0:T(8,128)}, u32[]{:S(2)}) copy-start(f32[128,1024]{1,0:T(8,128)} %get-tuple-element.31.middle) | copy-start | bytes 1572868
  187.6 13.1 %collective-permute-start = (f32[8,1024]{1,0:T(8,128)}, f32[8,1024]{1,0:T(8,128)S(1)}, u32[]{:S(2)}, u32[]{:S(2)}) collective-permute-start(f32[8,1024]{1,0:T(8,128)} %get-tuple-element.51), channel_id=1, source_target_pairs={{0,0},{1,16},{2,32},{3,48},{4,64},{5,80},{6,96},{7,112},{8,1},{9,1... | collective-permute-start | bytes 98312 | tf_op jit(solution)/shard_map/ppermute | solution.py:1036
  193.7 5.4 %copy-start.1 = (f32[2,64,1536]{2,1,0:T(8,128)S(1)}, f32[2,64,1536]{2,1,0:T(8,128)}, u32[]{:S(2)}) copy-start(f32[2,64,1536]{2,1,0:T(8,128)} %get-tuple-element.52) | copy-start | bytes 2359300

commit v2 on v1

--- a/solution.py
+++ b/solution.py
@@ -345,11 +345,12 @@
 
 def back_kernel(
     back, gates, normed, middle, cotangent, gain, small, out_own, context,
-    query, key2, value2, sums, cosine, sine, seg_column, seg_row, qkv_own, normed_one,
+    query, key2, value2, sums, cosine, sine, seg_row, qkv_own, normed_one,
     grads, mixed,
     grad_middle, grad_normed_one, bundle_all, out_sum, expert_grads, mixed_own,
     attended, attended_all, grad_context, grad_proj, grad_key, grad_value, blocks, small_part,
-    bundle, outp, bundle_in, out_in, bundle_sum, halves_a, halves_b,
+    bundle, outp, out_in, bundle_sum, halves_a, halves_b, hold_a, hold_b,
+    seg_column,
     *scratch,
 ):
     scratch = list(scratch)
@@ -373,7 +374,37 @@
     first_b = Quad("y", half_b, *take(5))
     second_a = Quad("y", lambda index, side: halves_a.at[side, index], *take(5))
     second_b = Quad("x", lambda index, side: halves_b.at[side, index], *take(5))
-    ring_send, ring_recv, s1, r1, s2, r2, s3, r3, loc = take(9)
+    quarter = bundle.shape[2] // 4
+
+    def bundle_a(index, side):
+        return bundle.at[:, index, pl.ds(side * quarter, quarter)]
+
+    def bundle_b(index, side):
+        return bundle.at[index, :, pl.ds((2 + side) * quarter, quarter)]
+
+    bundle_first = [Quad("x", bundle_a, *take(5)), Quad("y", bundle_b, *take(5))]
+    bundle_second = [
+        Quad("y", lambda index, side: hold_a.at[side, index], *take(5)),
+        Quad("x", lambda index, side: hold_b.at[side, index], *take(5)),
+    ]
+
+    def keep_bundle(hold):
+        def store(side, total):
+            hold[side] = total.astype(BF16)
+
+        return store
+
+    def store_bundle(first_row):
+        def store(side, total):
+            groups = quarter // bundle_sum.shape[1]
+            start = (first_row + side * quarter) // bundle_sum.shape[1]
+            bundle_sum[start : start + groups] = total.reshape(
+                groups, bundle_sum.shape[1], total.shape[1]
+            )
+
+        return store
+
+    ring_send, ring_recv, s2, r2, s3, r3, loc = take(7)
 
     def keep_a(side, total):
         halves_a[side] = total.astype(BF16)
@@ -385,6 +416,7 @@
     size = lax.axis_size("fsdp")
     first_a.start()
     first_b.start()
+    fill_column(seg_row, seg_column)
     width = cotangent.shape[1]
     value = middle[...]
     inverse = inverse_rms(value)
@@ -422,32 +454,38 @@
     )
     mix_scatter.near_blocks()
     span = grad_proj.shape[1]
-    share = bundle.shape[1]
-    tile = 256
+    share = bundle.shape[2]
+    tile = 4 * share
     for index in range(width // tile):
         at = slice(index * tile, (index + 1) * tile)
         part = dot(normed_one[:, at], grad_proj[...], ((0,), (0,))).astype(BF16)
-        place = slice(index * tile // share, (index + 1) * tile // share)
-        bundle[place, :, :span] = part.reshape(tile // share, share, span)
-        bundle[place, :, span:] = small_part[at, :].astype(BF16).reshape(tile // share, share, 128)
-    bundles = spread("fsdp", size, bundle, bundle_in, s1, r1, loc.at[2], True)
-    run(bundles)
+        bundle[index, :, :, :span] = part.reshape(tile // share, share, span)
+        bundle[index, :, :, span:] = (
+            small_part[at, :].astype(BF16).reshape(tile // share, share, 128)
+        )
+    for quad in bundle_first:
+        quad.start()
     for index in range(SP):
         at = slice(index * rows, (index + 1) * rows)
         blocks[index] = dot(grad_proj[at, :], qkv_own[...], ((1,), (1,))).astype(BF16)
     scatter.start()
+    for quad in bundle_first:
+        quad.near_blocks()
     first_a.end(keep_a)
     first_b.end(keep_b)
+    scatter.middle()
+    bundle_first[0].end(keep_bundle(hold_a))
+    bundle_first[1].end(keep_bundle(hold_b))
+    for quad in bundle_second:
+        quad.start()
     second_a.start()
     second_b.start()
-    scatter.middle()
     mix_scatter.end(mixed_own)
+    for quad in bundle_second:
+        quad.near_blocks()
     scatter.near_blocks()
-    settle(bundles)
-    total = bundle_in[0].astype(F32)
-    for index in range(1, size):
-        total = total + bundle_in[index].astype(F32)
-    bundle_sum[...] = total.reshape(bundle_sum.shape)
+    bundle_second[0].end(store_bundle(0))
+    bundle_second[1].end(store_bundle(2 * quarter))
     shares = spread("sp", SP, bundle_sum, bundle_all, s3, r3, loc.at[3], True)
     run(shares)
     second_a.near_blocks()
@@ -495,12 +533,29 @@
     return jnp.where(first_head((half, stacked.shape[1])), stacked[:half], stacked[half:])
 
 
+def row_to_column(row):
+    count = row.shape[1]
+    same = lax.broadcasted_iota(jnp.int32, (count, count), 0) == lax.broadcasted_iota(
+        jnp.int32, (count, count), 1
+    )
+    spread_row = jnp.broadcast_to(row.astype(F32), (count, count))
+    return jnp.sum(jnp.where(same, spread_row, 0.0), 1, keepdims=True)
+
+
+def fill_column(seg_row, seg_column):
+    for index in range(seg_row.shape[1] // 128):
+        at = slice(index * 128, (index + 1) * 128)
+        seg_column[at, :] = row_to_column(seg_row[:, at])
+
+
 def block_scores(block, query2, key2, seg_column, seg_row):
     lo, hi = block * BLOCK, (block + 1) * BLOCK
     k_lo = max(0, lo - LONGEST)
     rows = lo + lax.broadcasted_iota(jnp.int32, (BLOCK, hi - k_lo), 0)
     keys = k_lo + lax.broadcasted_iota(jnp.int32, (BLOCK, hi - k_lo), 1)
-    allowed = (keys <= rows) & (seg_column[lo:hi, :] == seg_row[:, k_lo:hi])
+    allowed = (keys <= rows) & (
+        seg_column[lo:hi, :] == seg_row[:, k_lo:hi].astype(F32)
+    )
     scores = dot(query2, key2[k_lo:hi, :], ((1,), (1,))) * HEAD_SIZE**-0.5
     return jnp.where(jnp.concatenate([allowed, allowed], 0), scores, -jnp.inf)
 
@@ -590,12 +645,12 @@
 
 
 def forward_kernel(
-    tokens, cotangent, top_idx, qkv, small, outw, expert_in, expert_out,
-    cosine, sine, seg_column, seg_row,
+    tokens, cotangent, top_idx, qkv, gain_one, gain_two, router, outw, expert_in, expert_out,
+    cosine, sine, seg_row,
     mid, out_mid, qkv_own, small_own, gains, normed_one, context, query, key2, value2, sums,
     out_own, normed_own, middle_own, gates_own, mixed, back, grads,
     packed, late, tokens_all, late_all, packed_all, out_all, w_buf, context_all, proj, normed,
-    acts, grad_acts, grad_results, blocks, middle_part, gates,
+    acts, grad_acts, grad_results, blocks, middle_part, gates, seg_column,
     *scratch,
 ):
     scratch = list(scratch)
@@ -635,6 +690,16 @@
             ),
         ]
     run(shard_copies)
+    fill_column(seg_row, seg_column)
+    lanes = lax.broadcasted_iota(jnp.int32, (qkv.shape[0], 128), 1)
+    shift = (
+        lax.broadcasted_iota(jnp.int32, (E, 128), 0) + 2
+        == lax.broadcasted_iota(jnp.int32, (E, 128), 1)
+    ).astype(F32).astype(BF16)
+    small = dot(router[...], shift, ((1,), (0,)))
+    small = small + jnp.where(lanes == 0, row_to_column(gain_one[...]), 0.0)
+    small = small + jnp.where(lanes == 1, row_to_column(gain_two[...]), 0.0)
+    small = small.astype(BF16)
     for index in range(SP):
         k_at = q_span + index * HEAD_SIZE
         packed[index, :, :group] = qkv[:, index * group : (index + 1) * group]
@@ -645,7 +710,7 @@
             ],
             1,
         )
-        packed[index, :, 2 * group :] = small[...]
+        packed[index, :, 2 * group :] = small
     own_rows = packed.shape[1]
 
     def rows_of(target):
@@ -731,7 +796,6 @@
                 sp=other,
             )
         )
-    run(sent)
     everything = packed_all[...].reshape(width, packed_all.shape[2])
     qkv_own[...] = everything[:, : 2 * group]
     small_own[...] = everything[:, 2 * group :]
@@ -752,15 +816,16 @@
     for quad in first:
         quad.forward()
     late_ring.forward()
-    attention_kernel(
-        proj, cosine, sine, seg_column, seg_row, context, query, key2, value2, sums
-    )
-    context_ring = ring_columns(context, context_all, s7, r7, loc.at[5])
-    context_ring.start()
+    run(sent)
     for quad in first:
         quad.close()
     for quad in second:
         quad.start()
+    attention_kernel(
+        proj, cosine, sine, seg_column, seg_row, context, query, key2, value2, sums
+    )
+    context_ring = ring_columns(context, context_all, s7, r7, loc.at[5])
+    context_ring.start()
     late_ring.close()
     for copy, onward in zip(sent, passed):
         copy.wait_recv()
@@ -771,6 +836,8 @@
         copy.wait_send()
     settle(passed)
     settle(keep)
+    for quad in second:
+        quad.forward()
     out_own[...] = out_all[pl.ds(2 * me, 2)].reshape(out_own.shape)
 
     def second_norm(index, carry):
@@ -787,8 +854,6 @@
         return carry
 
     lax.fori_loop(0, seq_len // chunk, second_norm, 0)
-    for quad in second:
-        quad.forward()
     middle_own[...] = middle_part[lax.rem(me, per_chunk)]
     at_own = pl.ds(pl.multiple_of(me * rows, rows), rows)
     normed_own[...] = normed[at_own, :]
@@ -911,12 +976,10 @@
     q_span, k_span = HQ * HEAD_SIZE, KEY_VALUE_HEADS * HEAD_SIZE
     group = q_span // n_sp
     head = k_span // n_sp
-    small = jnp.concatenate([norm1_gain[:, None], norm2_gain[:, None], router_weight], 1)
-    small = jnp.pad(small, ((0, 0), (0, 128 - small.shape[1])))
     pack_width = 2 * group + 128
     any_shape = jax.ShapeDtypeStruct
     cosine, sine = rope_tables(seq_len)
-    seg_row, seg_column = segments, segments.reshape(seq_len, 1)
+    seg_row = segments
     n_experts = expert_in.shape[0]
     in_span = expert_in.shape[2]
     slab = any_shape((seq_len, group), BF16)
@@ -928,10 +991,10 @@
         "forward",
         1,
         (
-            tokens, cotangent, top_idx, qkv_weight, small, out_weight, expert_in, expert_out,
-            cosine, sine, seg_column, seg_row,
+            tokens, cotangent, top_idx, qkv_weight, norm1_gain[None, :], norm2_gain[None, :],
+            router_weight, out_weight, expert_in, expert_out, cosine, sine, seg_row,
         ),
-        [HBM] + [VMEM] * 4 + [HBM] * 3 + [VMEM] * 4,
+        [HBM] + [VMEM] * 6 + [HBM] * 3 + [VMEM] * 3,
         (
             any_shape((SP * weight_rows, pack_width), BF16),
             any_shape((SP * weight_rows, width), BF16),
@@ -967,6 +1030,7 @@
             pltpu.VMEM((SP, rows, width + 128), BF16),
             pltpu.VMEM((2, rows, width), F32),
             pltpu.VMEM((seq_len, 128), F32),
+            pltpu.VMEM((seq_len, 1), F32),
         ]
         + scatter_scratch(rows, width + 128)
         + [DMA((8,))] * 6
@@ -988,11 +1052,11 @@
         4,
         (
             back, gates_own, normed_own, middle_own, cotangent, gain_two, small_own, out_own,
-            context, query, key2, value2, sums, cosine, sine, seg_column, seg_row, qkv_own,
+            context, query, key2, value2, sums, cosine, sine, seg_row, qkv_own,
             normed_one, grads.reshape(4, 4, n_experts, share, in_span + hidden),
             mixed.reshape(SP, rows, width),
         ),
-        [VMEM] * 21,
+        [VMEM] * 20,
         (
             any_shape((rows, width), F32),
             any_shape((rows, width), F32),
@@ -1011,19 +1075,23 @@
             pltpu.VMEM((seq_len, group), F32),
             pltpu.VMEM((SP, rows, width), BF16),
             pltpu.VMEM((width, 128), F32),
-            pltpu.VMEM((n_fsdp, share, pack_width), BF16),
+            pltpu.VMEM((4, 4, share, pack_width), BF16),
             pltpu.VMEM((n_fsdp, shares, width), BF16),
-            pltpu.VMEM((n_fsdp, share, pack_width), BF16),
             pltpu.VMEM((n_fsdp, shares, width), BF16),
             pltpu.VMEM((SP, weight_rows, pack_width), F32),
             pltpu.VMEM((2,) + half_grads, BF16),
             pltpu.VMEM((2,) + half_grads, BF16),
+            pltpu.VMEM((2, 4, share // 4, pack_width), BF16),
+            pltpu.VMEM((2, 4, share // 4, pack_width), BF16),
+            pltpu.VMEM((seq_len, 1), F32),
         ]
         + scatter_scratch(rows, width) * 2
         + quad_scratch(half_grads) * 2
         + quad_scratch(half_share) * 2
+        + quad_scratch((4, share // 4, pack_width)) * 2
+        + quad_scratch((share // 4, pack_width)) * 2
         + [DMA((8,))] * 2
-        + [DMA((n_fsdp,))] * 4
+        + [DMA((n_fsdp,))] * 2
         + [DMA((8,))] * 2
         + [DMA((4,))],
     )

time: 202 us -> 195 us (0.965)
  Pallas kernels: 180 us -> 176 us
  local copies, waits for them, and re-layouts: 10.6 us -> 7.46 us
    pallas_call x2, Pallas kernels: 180 us -> 176 us  [wide_call(): pl.pallas_call(kernel, name=name, out_shape=outs, in_specs=in_specs, out_...]
where the time goes in v2:
time: 195 us; the launch traced here: 194 us
  Pallas kernels  176 us (90%)
  local copies, waits for them, and re-layouts  7.46 us (4%)
  other arithmetic  5.9 us (3%)
  starting transfers between devices  4.19 us (2%)
    pallas_call x2, Pallas kernels, wide_call(): pl.pallas_call(kernel, name=name, out_shape=outs, in_specs=in_specs, out_...  176 us
    ppermute x1, starting transfers between devices, shards(): out_grad = lax.ppermute(out_sum, ('fsdp', 'sp'), moves)  4.19 us
  transfers between devices with their start and end apart: 1, of which 0 were waited for; matrix products, arithmetic and copies ran while one was open for 5% of the time, Pallas kernels for 0%

profile of v2, /device:TPU:1, one launch (start us, length us, event | category | flops | bytes accessed | tf_op | source)
XLA Modules:
  0.0 194.0 jit_solution(3939680223806085839)
XLA Ops:
  0.6 1.4 copy.23.top_idx
  2.1 114.2 %forward.1 = (bf16[64,384]{1,0:T(8,128)(2,1)}, bf16[64,1024]{1,0:T(8,128)(2,1)}, bf16[1024,256]{1,0:T(8,128)(2,1)}, bf16[1024,128]{1,0:T(8,128)(2,1)}, f32[8,102...) custom-call(bf16[128,1024]{1,0:T(8,128)(2,1)} %tokens.1, ...), custom_call_target="tpu_custom_call" | custom-call | flops 20000000000 | bytes 20000000 | tf_op jit(solution)/shard_map/forward/pallas_call | solution.py:940
  116.3 1.4 fusion.5
  117.7 0.0 copy-start
  117.7 0.0 copy-start.3
  117.7 0.0 copy-start.4
  117.7 0.0 copy-start.2
  117.7 61.5 %backward.1 = (f32[128,1024]{1,0:T(8,128)}, f32[128,1024]{1,0:T(8,128)}, f32[8,8,384]{2,1,0:T(8,128)}, f32[8,1024]{1,0:T(8,128)}, f32[2,64,1536]{2,1,0:T(8,128)}, /*index=5*/f32[128,1024]{1,0:T(8,128)}) custom-call(f32[128,1152]{1,0:T(8,128)} %get-tuple-element.32.back, f32[128,128]{1,0:T(8,128)} %get-tuple-element.33.gates, ...), custom_call_target="tpu_custom_call" | custom-call | flops 20000000000 | bytes 20000000 | tf_op jit(solution)/shard_map/backward/pallas_call | solution.py:940
  179.2 4.2 %collective-permute-start = (f32[8,1024]{1,0:T(8,128)}, f32[8,1024]{1,0:T(8,128)S(1)}, u32[]{:S(2)}, u32[]{:S(2)}) collective-permute-start(f32[8,1024]{1,0:T(8,128)} %get-tuple-element.51), channel_id=1, source_target_pairs={{0,0},{1,16},{2,32},{3,48},{4,64},{5,80},{6,96},{7,112},{8,1},{9,1... | collective-permute-start | bytes 98312 | tf_op jit(solution)/shard_map/ppermute | solution.py:1104
  183.4 0.8 slice_reduce_fusion
  184.2 0.9 slice_bitcast_fusion.1
  185.1 0.0 copy-done
  185.1 1.2 fusion
  186.4 0.0 copy-start.1
  186.4 0.1 reshape.54
  186.5 0.1 reshape.55
  186.6 0.0 copy-done.3
  186.6 0.7 multiply_reduce_fusion
  187.3 0.0 copy-done.4
  187.3 0.5 convert_divide_fusion
  187.9 0.0 copy-done.2
  187.9 2.6 %fusion.3 = (f32[128,1024]{1,0:T(8,128)}, f32[128,1024]{1,0:T(8,128)}) fusion(f32[128,1024]{1,0:T(8,128)} %get-tuple-element.48, bf16[128,1024]{1,0:T(8,128)(2,1)S(1)} %copy-done, f32[128,1024]{1,0:T(8,128)} %get-tuple-element.49, f32[128]{0:T(128)S(1)} %broadcast_multiply_fusion, f32[128]{0:T(128)S(1)} %get-tuple-element.64, f32[1024]{0:T(1024)S(1)} %bitcast.14, ...), kind=kLoop, calls=%fused_computation.6 | loop fusion | flops 1179648 | bytes 3413504 | tf_op jit(solution)/shard_map/add | solution.py:1126
  190.5 0.7 slice_reduce_fusion.1
  191.2 0.7 slice.37
  191.8 0.0 copy-done.1
  191.8 0.7 slice.39
  192.5 0.8 slice.38
  193.4 0.0 collective-permute-done
  193.4 0.6 copy.27
  (4 shorter events, 0.0 us)
Async XLA Ops:
  117.7 67.4 %copy-start = (bf16[128,1024]{1,0:T(8,128)(2,1)S(1)}, bf16[128,1024]{1,0:T(8,128)(2,1)}, u32[]{:S(2)}) copy-start(bf16[128,1024]{1,0:T(8,128)(2,1)} %tokens.1) | copy-start | bytes 786436
  117.7 68.9 %copy-start.3 = (bf16[8,2048]{1,0:T(8,128)(2,1)S(1)}, bf16[8,2048]{1,0:T(8,128)(2,1)}, u32[]{:S(2)}) copy-start(bf16[8,2048]{1,0:T(8,128)(2,1)} %qkv.1) | copy-start | bytes 98308
  117.7 69.6 %copy-start.4 = (bf16[8]{0:T(256)(128)(2,1)S(1)}, bf16[8]{0:T(256)(128)(2,1)}, u32[]{:S(2)}) copy-start(bf16[8]{0:T(256)(128)(2,1)} %param.17) | copy-start | bytes 52
  117.7 70.2 %copy-start.2 = (f32[128,1024]{1,0:T(8,128)S(1)}, f32[128,1024]{1,0:T(8,128)}, u32[]{:S(2)}) copy-start(f32[128,1024]{1,0:T(8,128)} %get-tuple-element.31.middle) | copy-start | bytes 1572868
  179.2 14.1 %collective-permute-start = (f32[8,1024]{1,0:T(8,128)}, f32[8,1024]{1,0:T(8,128)S(1)}, u32[]{:S(2)}, u32[]{:S(2)}) collective-permute-start(f32[8,1024]{1,0:T(8,128)} %get-tuple-element.51), channel_id=1, source_target_pairs={{0,0},{1,16},{2,32},{3,48},{4,64},{5,80},{6,96},{7,112},{8,1},{9,1... | collective-permute-start | bytes 98312 | tf_op jit(solution)/shard_map/ppermute | solution.py:1104
  186.4 5.4 %copy-start.1 = (f32[2,64,1536]{2,1,0:T(8,128)S(1)}, f32[2,64,1536]{2,1,0:T(8,128)}, u32[]{:S(2)}) copy-start(f32[2,64,1536]{2,1,0:T(8,128)} %get-tuple-element.52) | copy-start | bytes 2359300

commit v3 on v2

--- a/solution.py
+++ b/solution.py
@@ -344,11 +344,11 @@
 
 
 def back_kernel(
-    back, gates, normed, middle, cotangent, gain, small, out_own, context,
+    back, gates, normed, middle, tokens, cotangent, gain, small, out_own, context,
     query, key2, value2, sums, cosine, sine, seg_row, qkv_own, normed_one,
     grads, mixed,
-    grad_middle, grad_normed_one, bundle_all, out_sum, expert_grads, mixed_own,
-    attended, attended_all, grad_context, grad_proj, grad_key, grad_value, blocks, small_part,
+    block_out, input_grad, bundle_all, out_sum, expert_grads,
+    grad_middle, grad_normed_one, mixed_own, attended, attended_all, grad_context, grad_proj, grad_key, grad_value, blocks, small_part,
     bundle, outp, out_in, bundle_sum, halves_a, halves_b, hold_a, hold_b,
     seg_column,
     *scratch,
@@ -423,7 +423,9 @@
     weighted = back[:, width:]
     grad_logits = weighted - gates[...] * jnp.sum(weighted, -1, keepdims=True)
     grad_normed = back[:, :width] + exact_dot(grad_logits, small[...].astype(F32), ((1,), (1,)))
-    grad_rows = cotangent[...].astype(F32) + rms_backward(grad_normed, value, inverse, gain[...])
+    grad_rows = cotangent[...].astype(F32) + rms_backward(
+        grad_normed, value, inverse, gain[1:2, :]
+    )
     grad_middle[...] = grad_rows
     attended[...] = (RESIDUAL * grad_rows).astype(BF16)
     ring = ring_rows(attended, attended_all, ring_send, ring_recv, loc.at[0])
@@ -481,6 +483,7 @@
     second_a.start()
     second_b.start()
     mix_scatter.end(mixed_own)
+    block_out[...] = middle[...] + RESIDUAL * mixed_own[...]
     for quad in bundle_second:
         quad.near_blocks()
     scatter.near_blocks()
@@ -505,6 +508,10 @@
     second_a.end(store_a)
     second_b.end(store_b)
     scatter.end(grad_normed_one)
+    value = tokens[...].astype(F32)
+    input_grad[...] = grad_middle[...] + rms_backward(
+        grad_normed_one[...], value, inverse_rms(value), gain[0:1, :]
+    )
     settle(shares)
 
 
@@ -1041,32 +1048,33 @@
         + [DMA((12,))]
         + [DMA((4,))] * 8,
     )
-    gain_one, gain_two = gains[0:1], gains[1:2]
     share = width // n_fsdp
     shares = group // n_fsdp
     half_grads = (4, share // 2, in_span + hidden)
     half_share = (share // 2, in_span + hidden)
-    grad_middle, grad_normed_one, bundle, out_sum, expert_grads, mixed_own = wide_call(
+    block_out, input_grad, bundle, out_sum, expert_grads = wide_call(
         back_kernel,
         "backward",
         4,
         (
-            back, gates_own, normed_own, middle_own, cotangent, gain_two, small_own, out_own,
+            back, gates_own, normed_own, middle_own, tokens, cotangent, gains, small_own, out_own,
             context, query, key2, value2, sums, cosine, sine, seg_row, qkv_own,
             normed_one, grads.reshape(4, 4, n_experts, share, in_span + hidden),
             mixed.reshape(SP, rows, width),
         ),
-        [VMEM] * 20,
+        [VMEM] * 21,
         (
             any_shape((rows, width), F32),
             any_shape((rows, width), F32),
             any_shape((SP, weight_rows, pack_width), F32),
             any_shape((shares, width), F32),
             any_shape((n_experts, share, in_span + hidden), F32),
-            any_shape((rows, width), F32),
         ),
-        (VMEM,) * 6,
+        (VMEM,) * 5,
         [
+            pltpu.VMEM((rows, width), F32),
+            pltpu.VMEM((rows, width), F32),
+            pltpu.VMEM((rows, width), F32),
             pltpu.VMEM((rows, width), BF16),
             pltpu.VMEM((SP, rows, width), BF16),
             pltpu.VMEM((seq_len, group), BF16),
@@ -1095,7 +1103,6 @@
         + [DMA((8,))] * 2
         + [DMA((4,))],
     )
-    block_out = middle_own + RESIDUAL * mixed_own
     moves = []
     for f in range(n_fsdp):
         for s in range(n_sp):
@@ -1122,10 +1129,6 @@
     gain_two_grad = smalls[:, 1]
     router_grad = smalls[:, 2 : 2 + E]
     gain_one_grad = jnp.sum(qkv_grad * qkv_weight.astype(F32), 1) / norm1_gain.astype(F32)
-    hidden_own = tokens.astype(F32)
-    input_grad = grad_middle + rms_backward(
-        grad_normed_one, hidden_own, inverse_rms(hidden_own), gain_one
-    )
     return (
         block_out,
         input_grad,

time: 195 us -> 193 us (0.990)
  other arithmetic: 5.9 us -> 2.06 us
  local copies, waits for them, and re-layouts: 7.46 us -> 9.65 us
    add x1 -> x0, other arithmetic: 2.6 us -> none  [shards(): grad_middle + rms_backward(grad_normed_one, hidden_own, inverse_rms(hidde...]
  transfers between devices with their start and end apart: 1 -> 1, of which waited for: 0 -> 0; matrix products, arithmetic and copies ran while one was open for 5% -> 4% of each run, Pallas kernels for 0% -> 0%
where the time goes in v3:
time: 193 us
  Pallas kernels  176 us (91%)
  local copies, waits for them, and re-layouts  9.65 us (5%)
  starting transfers between devices  4.58 us (2%)
  other arithmetic  2.06 us (1%)
    pallas_call x2, Pallas kernels, wide_call(): pl.pallas_call(kernel, name=name, out_shape=outs, in_specs=in_specs, out_...  176 us
    ppermute x1, starting transfers between devices, shards(): out_grad = lax.ppermute(out_sum, ('fsdp', 'sp'), moves)  4.58 us
  transfers between devices with their start and end apart: 1, of which 0 were waited for; matrix products, arithmetic and copies ran while one was open for 4% of the time, Pallas kernels for 0%

profile of v3, /device:TPU:1, one launch (start us, length us, event | category | flops | bytes accessed | tf_op | source)
XLA Modules:
  0.0 192.6 jit_solution(14227587440681848694)
XLA Ops:
  0.6 1.4 copy.23.top_idx
  2.1 114.2 %forward.1 = (bf16[64,384]{1,0:T(8,128)(2,1)}, bf16[64,1024]{1,0:T(8,128)(2,1)}, bf16[1024,256]{1,0:T(8,128)(2,1)}, bf16[1024,128]{1,0:T(8,128)(2,1)}, f32[8,102...) custom-call(bf16[128,1024]{1,0:T(8,128)(2,1)} %tokens.3, ...), custom_call_target="tpu_custom_call" | custom-call | flops 20000000000 | bytes 20000000 | tf_op jit(solution)/shard_map/forward/pallas_call | solution.py:947
  116.3 0.0 copy-start.2
  116.3 0.0 copy-start.3
  116.3 61.4 %backward.1 = (f32[128,1024]{1,0:T(8,128)}, f32[128,1024]{1,0:T(8,128)}, f32[8,8,384]{2,1,0:T(8,128)}, f32[8,1024]{1,0:T(8,128)}, f32[2,64,1536]{2,1,0:T(8,128)}) custom-call(f32[128,1152]{1,0:T(8,128)} %get-tuple-element.30.back, f32[128,128]{1,0:T(8,128)} %get-tuple-element.31.gates, bf16[128,1024]{1,0:T(8,128)(2,1)} %get-tuple-element.32.normed, ...), custom_call_target="tpu_custom_call" | custom-call | flops 20000000000 | bytes 20000000 | tf_op jit(solution)/shard_map/backward/pallas_call | solution.py:947
  177.7 0.0 copy-start.1
  177.7 0.0 copy-start
  177.7 4.6 %collective-permute-start = (f32[8,1024]{1,0:T(8,128)}, f32[8,1024]{1,0:T(8,128)S(1)}, u32[]{:S(2)}, u32[]{:S(2)}) collective-permute-start(f32[8,1024]{1,0:T(8,128)} %get-tuple-element.49), channel_id=1, source_target_pairs={{0,0},{1,16},{2,32},{3,48},{4,64},{5,80},{6,96},{7,112},{8,1},{9,1... | collective-permute-start | bytes 98312 | tf_op jit(solution)/shard_map/ppermute | solution.py:1111
  182.3 0.8 slice_reduce_fusion
  183.1 0.9 slice_bitcast_fusion.1
  184.0 0.1 reshape.36
  184.1 0.1 reshape.37
  184.2 0.0 copy-done.2
  184.2 0.7 multiply_reduce_fusion
  184.9 0.0 copy-done.3
  184.9 0.5 convert_divide_fusion
  185.5 0.7 slice_reduce_fusion.1
  186.2 0.7 slice.29
  186.8 1.7 slice.31
  188.5 1.9 slice.30
  190.4 0.0 collective-permute-done
  190.4 0.0 copy-done.1
  190.4 0.8 copy.29
  191.2 0.0 copy-done
  191.2 0.8 copy.30
  192.0 0.6 copy.31
  (2 shorter events, 0.0 us)
Async XLA Ops:
  116.3 67.9 %copy-start.2 = (bf16[8,2048]{1,0:T(8,128)(2,1)S(1)}, bf16[8,2048]{1,0:T(8,128)(2,1)}, u32[]{:S(2)}) copy-start(bf16[8,2048]{1,0:T(8,128)(2,1)} %qkv.1) | copy-start | bytes 98308
  116.3 68.7 %copy-start.3 = (bf16[8]{0:T(256)(128)(2,1)S(1)}, bf16[8]{0:T(256)(128)(2,1)}, u32[]{:S(2)}) copy-start(bf16[8]{0:T(256)(128)(2,1)} %param.17) | copy-start | bytes 52
  177.7 12.7 %copy-start.1 = (f32[128,1024]{1,0:T(8,128)S(1)}, f32[128,1024]{1,0:T(8,128)}, u32[]{:S(2)}) copy-start(f32[128,1024]{1,0:T(8,128)} %get-tuple-element.66) | copy-start | bytes 1572868
  177.7 13.5 %copy-start = (f32[128,1024]{1,0:T(8,128)S(1)}, f32[128,1024]{1,0:T(8,128)}, u32[]{:S(2)}) copy-start(f32[128,1024]{1,0:T(8,128)} %get-tuple-element.67) | copy-start | bytes 1572868
  177.7 12.7 %collective-permute-start = (f32[8,1024]{1,0:T(8,128)}, f32[8,1024]{1,0:T(8,128)S(1)}, u32[]{:S(2)}, u32[]{:S(2)}) collective-permute-start(f32[8,1024]{1,0:T(8,128)} %get-tuple-element.49), channel_id=1, source_target_pairs={{0,0},{1,16},{2,32},{3,48},{4,64},{5,80},{6,96},{7,112},{8,1},{9,1... | collective-permute-start | bytes 98312 | tf_op jit(solution)/shard_map/ppermute | solution.py:1111
